TPU v7x, 512 devices: a whole 4x4x16 slice. The times are simulated.
512 devices in a mesh: dp: 16 (over x, y), expert: 32 (over z, core).
Axes of the slice: x: 4, y: 4, z: 16, core: 2. Of those that a mesh axis runs over, the one named last changes fastest.
Arguments:
- tokens: bfloat16 [8192, 1024], P(('dp', 'expert')), may hold values from -6 to 6
- upstream: bfloat16 [8192, 1024], P(('dp', 'expert')), may hold values from -6 to 6
- expert_ids: int32 [8192, 8], P(('dp', 'expert')), may hold values from 0 to 127, all different within a row; in each aligned block of 16 rows (0 to 15, 16 to 31, ...) at most 2 rows name the same one
- gates: float32 [8192, 8], P(('dp', 'expert')), may hold values from 0.05 to 1
- relocate: int32 [32, 4], replicated, may hold values from 0 to 1, as said below
- w_gate_up: bfloat16 [32, 16, 384, 1024], P('expert', 'dp'), may hold values from -0.1875 to 0.1875
- w_down: bfloat16 [32, 16, 192, 1024], P('expert', 'dp'), may hold values from -0.21875 to 0.21875
Outputs:
- grad_tokens: bfloat16 [8192, 1024], P(('dp', 'expert'))
- grad_gate_up: bfloat16 [32, 16, 384, 1024], P('expert', 'dp')
- grad_down: bfloat16 [32, 16, 192, 1024], P('expert', 'dp')
Inputs may be any that keep to these rules, and one draw needn't show every extreme that they name: `expert_ids`: each row names 8 different experts; the rows of one device name one expert at most 2 times, and some device reaches 2. `relocate`: the first and the second half of the rows are equal; both values occur.
All inputs are finite; a program needn't handle non-finite values.
Results may differ from a plain program's by a relative error of at most 0.0064.
Values may be sent and summed in bfloat16 or wider, within the bound.
A program may use at most 64 MiB of HBM per device.

v0:
```python
import jax
import jax.numpy as jnp
from jax import lax
from jax.sharding import PartitionSpec as P

SLICES = 4


contract_last = (((1,), (1,)), ((), ()))
contract_first = (((0,), (0,)), ((), ()))


def swapped(block, axis, apart):
    count = lax.axis_size(axis)
    route = []
    for low in range(count):
        high = low | 1 << apart
        if high != low and high < count:
            route += [(low, high), (high, low)]
    return lax.ppermute(block, axis, route)


def silu_parts(values_in):
    sigmoid_of = jax.nn.sigmoid(values_in)
    return (values_in * sigmoid_of, sigmoid_of * (1.0 + values_in * (1.0 - sigmoid_of)))


def pick_entry(lookup_table, row_index, col_index):
    rows_hit = jnp.arange(lookup_table.shape[0], dtype=jnp.int32)[:, None] == row_index
    cols_hit = jnp.arange(lookup_table.shape[1], dtype=jnp.int32)[None, :] == col_index
    return jnp.sum(jnp.where(rows_hit & cols_hit, lookup_table, 0))


def per_device(tokens, upstream, expert_ids, gates, relocate, w_gate_up, w_down):
    n_rows = lax.axis_size("dp")
    n_cols = lax.axis_size("expert")
    slot_count = n_rows // SLICES
    experts = slot_count * n_cols
    tok_dev, feature_width = tokens.shape
    top_count = expert_ids.shape[1]
    capacity = min(tok_dev, max(2, (3 * tok_dev * top_count + 2 * experts - 1) // (2 * experts)))
    pair_count = tok_dev * top_count
    buffer_rows = experts * capacity
    slice_width = w_down.shape[2]
    col_block = n_cols // SLICES
    col_here = lax.axis_index("expert")
    row_here = lax.axis_index("dp")
    slot_here = row_here // SLICES
    slice_here = row_here % SLICES
    far_bit = n_cols.bit_length() - 2
    half_cols = n_cols // 2
    flat_ids = expert_ids.reshape(pair_count)
    home_column = flat_ids // slot_count
    slot_of = flat_ids % slot_count
    expert_iota = jnp.arange(experts, dtype=jnp.int32)
    relocated = jnp.sum(
        jnp.where(flat_ids[:, None] == expert_iota[None, :], relocate.reshape(experts)[None, :], 0),
        axis=1,
    )
    column = (home_column + half_cols * relocated) % n_cols
    pair_iota = jnp.arange(pair_count, dtype=jnp.int32)
    earlier = (flat_ids[:, None] == flat_ids[None, :]) & (pair_iota[None, :] < pair_iota[:, None])
    slot_rank = jnp.sum(earlier.astype(jnp.int32), axis=1)
    target = (slot_of * n_cols + column) * capacity + slot_rank
    placing = (target[None, :] == jnp.arange(buffer_rows, dtype=jnp.int32)[:, None]).astype(
        jnp.bfloat16
    )
    x_pairs = jnp.repeat(tokens, top_count, axis=0)
    d_pairs = (
        gates.reshape(pair_count, 1) * jnp.repeat(upstream, top_count, axis=0).astype(jnp.float32)
    ).astype(jnp.bfloat16)
    pair_data = jnp.stack([x_pairs, d_pairs])
    sent = jnp.einsum("bp,kpw->kbw", placing, pair_data, preferred_element_type=jnp.float32).astype(
        jnp.bfloat16
    )
    sent = sent.reshape(2, slot_count, n_cols, capacity, feature_width)
    at_column = lax.all_to_all(sent, "expert", split_axis=2, concat_axis=2, tiled=True)
    swapped_here = pick_entry(relocate, col_here, slot_here)
    own_pack = jnp.concatenate([w_gate_up, w_down], axis=2)
    far_pack = swapped(own_pack, "expert", far_bit)
    own_pack = jnp.where(swapped_here == 1, far_pack, own_pack)
    gate_up = own_pack[0, 0, : 2 * slice_width]
    down_rows = own_pack[0, 0, 2 * slice_width :]
    grouped = at_column.reshape(2, n_rows, col_block, capacity, feature_width)
    at_row = lax.all_to_all(grouped, "dp", split_axis=1, concat_axis=1, tiled=True)
    gathered = at_row[:, None]
    for bit_index in range(SLICES.bit_length() - 1):
        far_rows = swapped(gathered, "dp", bit_index)
        lower_half = slice_here // (1 << bit_index) % 2 == 0
        first_part = jnp.where(lower_half, gathered, far_rows)
        second_part = jnp.where(lower_half, far_rows, gathered)
        gathered = jnp.concatenate([first_part, second_part], axis=1)
    all_rows = gathered.reshape(2, -1, feature_width)
    rows_x = all_rows[0]
    rows_d = all_rows[1]
    gate_and_up = lax.dot_general(
        rows_x, gate_up, contract_last, preferred_element_type=jnp.float32
    )
    gate_pre = gate_and_up[:, :slice_width]
    up_pre = gate_and_up[:, slice_width:]
    activated, slope_of = silu_parts(gate_pre)
    hidden = (activated * up_pre).astype(jnp.bfloat16)
    hidden_grad = lax.dot_general(
        rows_d, down_rows, contract_last, preferred_element_type=jnp.float32
    )
    pre_grads = jnp.concatenate(
        [
            (hidden_grad * up_pre * slope_of).astype(jnp.bfloat16),
            (hidden_grad * activated).astype(jnp.bfloat16),
        ],
        axis=1,
    )
    grad_gu = lax.dot_general(
        pre_grads, rows_x, contract_first, preferred_element_type=jnp.float32
    ).astype(jnp.bfloat16)
    grad_dn = lax.dot_general(
        hidden, rows_d, contract_first, preferred_element_type=jnp.float32
    ).astype(jnp.bfloat16)
    slice_part = jnp.dot(pre_grads, gate_up, preferred_element_type=jnp.float32).astype(
        jnp.bfloat16
    )
    grad_pack = jnp.concatenate([grad_gu, grad_dn], axis=0)
    blocks = slice_part.reshape(2, 2, n_rows, col_block, capacity, feature_width)
    upper_half = slice_here // 2 % 2 == 1
    keep_half = jnp.where(upper_half, blocks[1], blocks[0])
    send_half = jnp.where(upper_half, blocks[0], blocks[1])
    got_half = swapped(send_half, "dp", 1)
    pairsum = keep_half.astype(jnp.float32) + got_half.astype(jnp.float32)
    odd_slice = slice_here % 2 == 1
    keep_last = jnp.where(odd_slice, pairsum[1], pairsum[0])
    send_last = jnp.where(odd_slice, pairsum[0], pairsum[1])
    got_last = swapped(send_last, "dp", 0)
    summed = keep_last + got_last
    back_rows = lax.all_to_all(summed, "dp", split_axis=0, concat_axis=0, tiled=True).reshape(
        slot_count, n_cols, capacity, feature_width
    )
    home_rows = lax.all_to_all(
        back_rows, "expert", split_axis=1, concat_axis=1, tiled=True
    ).reshape(buffer_rows, feature_width)
    hits = (
        target.reshape(tok_dev, top_count)[:, :, None]
        == jnp.arange(buffer_rows, dtype=jnp.int32)[None, None, :]
    )
    gather_mat = jnp.sum(hits.astype(jnp.float32), axis=1)
    grad_tokens = jnp.dot(
        gather_mat, home_rows, precision=lax.Precision.HIGHEST, preferred_element_type=jnp.float32
    ).astype(jnp.bfloat16)
    grad_gate_up = grad_pack[: 2 * slice_width].reshape(w_gate_up.shape)
    grad_down = grad_pack[2 * slice_width :].reshape(w_down.shape)
    return (grad_tokens, grad_gate_up, grad_down)


def solution(mesh):
    return jax.shard_map(
        per_device,
        mesh=mesh,
        in_specs=(
            P(("dp", "expert"), None),
            P(("dp", "expert"), None),
            P(("dp", "expert"), None),
            P(("dp", "expert"), None),
            P(),
            P("expert", "dp", None, None),
            P("expert", "dp", None, None),
        ),
        out_specs=(
            P(("dp", "expert"), None),
            P("expert", "dp", None, None),
            P("expert", "dp", None, None),
        ),
        check_vma=False,
    )
```

profile of v0, /device:TPU:1, one launch (start us, length us, event | category | flops | bytes accessed | tf_op | source)
XLA Modules:
  0.0 423.3 jit_solution(11939409705777303635)
XLA Ops:
  0.6 0.0 copy-start
  0.6 0.8 copy.61
  1.4 0.1 eq.100
  1.5 0.8 copy.66
  2.3 0.1 broadcast_in_dim.35
  2.4 0.8 convert_element_type.69
  3.1 0.8 copy.67
  3.9 0.1 mul.87
  4.0 0.2 select_reduce_fusion
  4.2 0.1 fusion.9
  4.3 0.4 fusion.1
  4.8 0.4 reshape.226
  5.2 1.1 copy.68
  6.4 72.2 %all_to_all.20 = bf16[2,4,32,2,1024]{4,3,1,0,2:T(2,128)(2,1)S(1)} all-to-all(bf16[2,4,32,2,1024]{4,3,1,0,2:T(2,128)(2,1)S(1)} %copy.68), channel_id=1, replica_groups=mesh['dp'=16,'expert'=32] {'expert'}, dimensions={2} | all-to-all | bytes 2097152 | tf_op jit(solution)/shard_map/all_to_all | solution.py:77
  78.6 0.6 copy.69
  79.2 1.1 copy.70
  80.2 22.5 %all_to_all.21 = bf16[2,16,8,2,1024]{4,3,2,0,1:T(2,128)(2,1)S(1)} all-to-all(bf16[2,16,8,2,1024]{4,3,2,0,1:T(2,128)(2,1)S(1)} %copy.70), channel_id=1, replica_groups=mesh['dp'=16,'expert'=32] {'dp'}, dimensions={1} | all-to-all | bytes 2097152 | tf_op jit(solution)/shard_map/all_to_all | solution.py:85
  102.7 2.5 collective-permute-start
  105.2 22.3 %collective-permute-done = bf16[2,1,16,8,2,1024]{5,4,3,0,2,1:T(2,128)(2,1)} collective-permute-done((bf16[2,1,16,8,2,1024]{5,4,3,0,2,1:T(2,128)(2,1)S(1)}, bf16[2,1,16,8,2,1024]{5,4,3,0,2,1:T(2,128)(2,1)}, u32[]{:S(2)}, u32[]{:S(2)}) %collective-permute-start) | collective-permute-done | bytes 1048608 | tf_op jit(solution)/shard_map/ppermute | solution.py:20
  127.6 2.8 broadcast_select_fusion.3
  130.4 0.0 copy-start.5
  130.4 0.0 copy-start.6
  130.4 4.4 %pad_maximum_fusion.1 = bf16[2,2,16,8,2,1024]{5,4,3,0,2,1:T(2,128)(2,1)} fusion(bf16[2,1,16,8,2,1024]{5,4,3,0,2,1:T(2,128)(2,1)S(1)} %get-tuple-element.14, bf16[2,1,16,8,2,1024]{5,4,3,0,2,1:T(2,128)(2,1)S(1)} %get-tuple-element.13), kind=kLoop, calls=%fused_computation.6 | loop fusion | flops 1048576 | bytes 4194304 | tf_op jit(solution)/shard_map/concatenate | solution.py:92
  134.8 3.4 collective-permute-start.1
  138.2 0.1 constant_dynamic-update-slice_fusion.1
  138.3 4.7 %collective-permute-start.2 = (bf16[1,1,576,1024]{3,2,1,0:T(8,128)(2,1)S(1)}, bf16[1,1,576,1024]{3,2,1,0:T(8,128)(2,1)}, u32[]{:S(2)}, u32[]{:S(2)}) collective-permute-start(bf16[1,1,576,1024]{3,2,1,0:T(8,128)(2,1)S(1)} %constant_dynamic-update-slice_fusion), channel_id=1, source_target_pairs={{0,16},{16,0},{1,17},{17,1},{2,18},{18,2},{3,19},{19,3},{4,20},{20... | collective-permute-start | bytes 3538952 | tf_op jit(solution)/shard_map/ppermute | solution.py:20
  143.2 0.0 copy-done.7
  143.2 0.7 select_reduce_fusion.1
  144.5 87.8 %collective-permute-done.2 = bf16[1,1,576,1024]{3,2,1,0:T(8,128)(2,1)} collective-permute-done((bf16[1,1,576,1024]{3,2,1,0:T(8,128)(2,1)S(1)}, bf16[1,1,576,1024]{3,2,1,0:T(8,128)(2,1)}, u32[]{:S(2)}, u32[]{:S(2)}) %collective-permute-start.2) | collective-permute-done | bytes 1179680 | tf_op jit(solution)/shard_map/ppermute | solution.py:20
  232.3 1.2 broadcast_select_fusion.4
  233.5 0.0 collective-permute-done.1
  233.5 6.1 %broadcast_select_fusion = (bf16[2,2,16,8,2,1024]{5,4,3,0,2,1:T(2,128)(2,1)S(1)}, bf16[2,2,16,8,2,1024]{5,4,3,0,2,1:T(2,128)(2,1)S(1)}) fusion(bf16[2,2,16,8,2,1024]{5,4,3,0,2,1:T(2,128)(2,1)} %collective-permute-done.1, pred[]{:T(512)S(6)} %eq.112, bf16[2,1,16,8,2,1024]{5,4,3,0,2,1:T(2,128)(2,1)S(1)} %get-tuple-element.14, ...), kind=kLoop, calls=%fused_computation.2 | loop fusion | flops 3145728 | bytes 8388609 | tf_op jit(solution)/shard_map/jit(_where)/select_n | solution.py:91
  239.5 6.3 %pad_maximum_fusion = (bf16[1,4,16,8,2,1024]{5,4,3,0,2,1:T(2,128)(2,1)}, bf16[1,4,16,8,2,1024]{5,4,3,0,2,1:T(2,128)(2,1)S(1)}) fusion(bf16[2,2,16,8,2,1024]{5,4,3,0,2,1:T(2,128)(2,1)S(1)} %get-tuple-element.7, bf16[2,2,16,8,2,1024]{5,4,3,0,2,1:T(2,128)(2,1)S(1)} %get-tuple-element.8), kind=kLoop, calls=%fused_computation.5 | loop fusion | flops 2097152 | bytes 8388608 | tf_op jit(solution)/shard_map/concatenate | solution.py:92
  245.8 4.1 squeeze.10
  249.9 2.2 squeeze.8
  252.1 2.7 fusion.5
  254.9 0.0 copy-done.1
  254.9 1.1 multiply_convert_fusion.2
  256.0 0.1 copy-done.8
  256.1 1.3 convolution_convert_fusion
  257.4 1.2 broadcast_select_fusion.5
  258.6 1.5 select_n.166
  260.0 1.3 copy.71
  261.3 1.9 collective-permute-start.3
  263.3 2.3 reshape.232
  265.6 23.5 %collective-permute-done.3 = bf16[2,16,8,2,1024]{4,2,3,1,0:T(8,128)(2,1)S(1)} collective-permute-done((bf16[2,16,8,2,1024]{4,2,3,1,0:T(8,128)(2,1)}, bf16[2,16,8,2,1024]{4,2,3,1,0:T(8,128)(2,1)S(1)}, u32[]{:S(2)}, u32[]{:S(2)}) %collective-permute-start.3) | collective-permute-done | bytes 1048608 | tf_op jit(solution)/shard_map/ppermute | solution.py:20
  289.0 2.6 copy_add_fusion
  291.6 0.1 select_bitcast_fusion
  291.8 3.3 collective-permute-start.4
  295.1 21.8 %collective-permute-done.4 = f32[16,8,2,1024]{3,1,2,0:T(8,128)S(1)} collective-permute-done((f32[16,8,2,1024]{3,1,2,0:T(8,128)S(1)}, f32[16,8,2,1024]{3,1,2,0:T(8,128)S(1)}, u32[]{:S(2)}, u32[]{:S(2)}) %collective-permute-start.4) | collective-permute-done | bytes 1048608 | tf_op jit(solution)/shard_map/ppermute | solution.py:20
  316.9 0.3 bitcast_add_fusion
  317.2 20.0 %all_to_all.22 = f32[16,8,2,1024]{3,1,2,0:T(8,128)S(1)} all-to-all(f32[16,8,2,1024]{3,1,2,0:T(8,128)S(1)} %bitcast_add_fusion), channel_id=1, replica_groups=mesh['dp'=16,'expert'=32] {'dp'}, dimensions={0} | all-to-all | bytes 2097152 | tf_op jit(solution)/shard_map/all_to_all | solution.py:134
  337.2 0.1 copy.73
  337.3 1.8 copy.74
  339.1 26.5 %all-to-all-start.3 = ((f32[4,32,2,1024]{3,2,0,1:T(2,128)}), f32[4,32,2,1024]{3,2,0,1:T(2,128)S(1)}, u32[]{:S(2)}, u32[]{:S(2)}) async-start(f32[4,32,2,1024]{3,2,0,1:T(2,128)} %copy.74), calls=%async_computation.3 | async-start | bytes 2097152 | tf_op jit(solution)/shard_map/all_to_all | solution.py:137
  365.6 0.1 reduce_sum.40
  365.7 0.1 mul.85
  365.8 0.1 convert_reduce_fusion
  365.9 3.1 fusion.2
  369.1 1.4 fusion.3
  370.4 50.8 %all-to-all-done.3 = f32[4,32,2,1024]{3,2,0,1:T(2,128)S(1)} async-done(((f32[4,32,2,1024]{3,2,0,1:T(2,128)}), f32[4,32,2,1024]{3,2,0,1:T(2,128)S(1)}, u32[]{:S(2)}, u32[]{:S(2)}) %all-to-all-start.3) | async-done | bytes 1048608 | tf_op jit(solution)/shard_map/all_to_all | solution.py:137
  421.3 0.1 copy.75
  421.4 0.7 reshape.229
  422.1 1.2 convolution_convert_fusion.4
  (24 shorter events, 0.2 us)
Async XLA Ops:
  0.6 3.4 copy-start
  102.7 24.8 %collective-permute-start = (bf16[2,1,16,8,2,1024]{5,4,3,0,2,1:T(2,128)(2,1)S(1)}, bf16[2,1,16,8,2,1024]{5,4,3,0,2,1:T(2,128)(2,1)}, u32[]{:S(2)}, u32[]{:S(2)}) collective-permute-start(bf16[2,1,16,8,2,1024]{5,4,3,0,2,1:T(2,128)(2,1)S(1)} %bitcast.43), channel_id=1, source_target_pairs={{0,32},{32,0},{64,96},{96,64},{128,160},{160,128},{192,224},{224,1... | collective-permute-start | bytes 3145736 | tf_op jit(solution)/shard_map/ppermute | solution.py:20
  130.4 7.8 %copy-start.5 = (bf16[1,1,384,1024]{3,2,1,0:T(8,128)(2,1)S(1)}, bf16[1,1,384,1024]{3,2,1,0:T(8,128)(2,1)}, u32[]{:S(2)}) copy-start(bf16[1,1,384,1024]{3,2,1,0:T(8,128)(2,1)} %param.12) | copy-start | bytes 2359300
  130.4 7.9 %copy-start.6 = (bf16[1,1,192,1024]{3,2,1,0:T(8,128)(2,1)S(1)}, bf16[1,1,192,1024]{3,2,1,0:T(8,128)(2,1)}, u32[]{:S(2)}) copy-start(bf16[1,1,192,1024]{3,2,1,0:T(8,128)(2,1)} %param.13) | copy-start | bytes 1179652
  134.8 8.3 %copy-start.7 = (s32[32,4]{0,1:T(4,128)S(1)}, s32[32,4]{0,1:T(4,128)}, u32[]{:S(2)}) copy-start(s32[32,4]{0,1:T(4,128)} %param.11) | copy-start | bytes 1540
  134.8 98.6 %collective-permute-start.1 = (bf16[2,2,16,8,2,1024]{5,4,3,0,2,1:T(2,128)(2,1)}, bf16[2,2,16,8,2,1024]{5,4,3,0,2,1:T(2,128)(2,1)}, u32[]{:S(2)}, u32[]{:S(2)}) collective-permute-start(bf16[2,2,16,8,2,1024]{5,4,3,0,2,1:T(2,128)(2,1)} %pad_maximum_fusion.1), channel_id=1, source_target_pairs={{0,64},{64,0},{32,96},{96,32},{128,192},{192,128},{160,224},{224,1... | collective-permute-start | bytes 6291464 | tf_op jit(solution)/shard_map/ppermute | solution.py:20
  138.3 94.0 %collective-permute-start.2 = (bf16[1,1,576,1024]{3,2,1,0:T(8,128)(2,1)S(1)}, bf16[1,1,576,1024]{3,2,1,0:T(8,128)(2,1)}, u32[]{:S(2)}, u32[]{:S(2)}) collective-permute-start(bf16[1,1,576,1024]{3,2,1,0:T(8,128)(2,1)S(1)} %constant_dynamic-update-slice_fusion), channel_id=1, source_target_pairs={{0,16},{16,0},{1,17},{17,1},{2,18},{18,2},{3,19},{19,3},{4,20},{20... | collective-permute-start | bytes 3538952 | tf_op jit(solution)/shard_map/ppermute | solution.py:20
  249.9 2.2 copy-start.4
  252.1 2.8 copy-start.1
  254.9 1.2 copy-start.8
  256.1 1.3 copy-start.10
  256.1 1.3 copy-start.11
  261.3 27.7 %collective-permute-start.3 = (bf16[2,16,8,2,1024]{4,2,3,1,0:T(8,128)(2,1)}, bf16[2,16,8,2,1024]{4,2,3,1,0:T(8,128)(2,1)S(1)}, u32[]{:S(2)}, u32[]{:S(2)}) collective-permute-start(bf16[2,16,8,2,1024]{4,2,3,1,0:T(8,128)(2,1)} %copy.71), channel_id=1, source_target_pairs={{0,64},{64,0},{32,96},{96,32},{128,192},{192,128},{160,224},{224,1... | collective-permute-start | bytes 3145736 | tf_op jit(solution)/shard_map/ppermute | solution.py:20
  291.8 25.1 %collective-permute-start.4 = (f32[16,8,2,1024]{3,1,2,0:T(8,128)S(1)}, f32[16,8,2,1024]{3,1,2,0:T(8,128)S(1)}, u32[]{:S(2)}, u32[]{:S(2)}) collective-permute-start(f32[16,8,2,1024]{3,1,2,0:T(8,128)S(1)} %select_bitcast_fusion), channel_id=1, source_target_pairs={{0,32},{32,0},{64,96},{96,64},{128,160},{160,128},{192,224},{224,1... | collective-permute-start | bytes 3145736 | tf_op jit(solution)/shard_map/ppermute | solution.py:20
  337.3 28.6 %copy-start.3 = (bf16[1024,1024]{1,0:T(8,128)(2,1)S(1)}, bf16[1024,1024]{1,0:T(8,128)(2,1)}, u32[]{:S(2)}) copy-start(bf16[1024,1024]{1,0:T(8,128)(2,1)} %squeeze.10) | copy-start | bytes 6291460
  339.1 82.2 %all-to-all-start.3 = ((f32[4,32,2,1024]{3,2,0,1:T(2,128)}), f32[4,32,2,1024]{3,2,0,1:T(2,128)S(1)}, u32[]{:S(2)}, u32[]{:S(2)}) async-start(f32[4,32,2,1024]{3,2,0,1:T(2,128)} %copy.74), calls=%async_computation.3 | async-start | bytes 2097152 | tf_op jit(solution)/shard_map/all_to_all | solution.py:137
  365.9 3.1 copy-start.2
  365.9 3.1 copy-start.9
where the time goes:
time: 424 us; the launch traced here: 423 us
  waiting for transfers between devices  206 us (49%)
  blocking collectives  115 us (27%)
  starting transfers between devices  42.3 us (10%)
  other arithmetic  26.9 us (6%)
  local copies, waits for them, and re-layouts  20.2 us (5%)
  matrix products  11.3 us (3%)
    ppermute x5, waiting for transfers between devices, swapped(): return lax.ppermute(block, axis, route)  155 us
    all_to_all x1, blocking collectives, per_device(): lax.all_to_all(sent, 'expert', split_axis=2, concat_axis=2, tiled=True)  72.2 us
    all_to_all x1, waiting for transfers between devices, per_device(): lax.all_to_all(back_rows, 'expert', split_axis=1, concat_axis=1, tiled=True)  50.8 us
    all_to_all x1, starting transfers between devices, per_device(): lax.all_to_all(back_rows, 'expert', split_axis=1, concat_axis=1, tiled=True)  26.5 us
    all_to_all x1, blocking collectives, per_device(): lax.all_to_all(grouped, 'dp', split_axis=1, concat_axis=1, tiled=True)  22.5 us
    all_to_all x1, blocking collectives, per_device(): lax.all_to_all(summed, 'dp', split_axis=0, concat_axis=0, tiled=True)  20 us
    ppermute x5, starting transfers between devices, swapped(): return lax.ppermute(block, axis, route)  15.8 us
    concatenate x2, other arithmetic, per_device(): gathered = jnp.concatenate([first_part, second_part], axis=1)  10.7 us
  transfers between devices with their start and end apart: 6, of which 5 were waited for; matrix products, arithmetic and copies ran while one was open for 2% of the time, Pallas kernels for 0%

commit v1 on v0

v1 whole, which is shorter than its diff:
```python
import jax
import jax.numpy as jnp
from jax import lax
from jax.sharding import PartitionSpec as P

SLICES = 4
CAP = 2

contract_last = (((1,), (1,)), ((), ()))
contract_first = (((0,), (0,)), ((), ()))


def silu_parts(values_in):
    sigmoid_of = jax.nn.sigmoid(values_in)
    return (values_in * sigmoid_of, sigmoid_of * (1.0 + values_in * (1.0 - sigmoid_of)))


def half_swap(block, count, parity):
    half = count // 2
    route = [(c, (c + half) % count) for c in range(count) if c % 2 == parity]
    return lax.ppermute(block, "expert", route)


def three_parts(gates):
    first = lax.reduce_precision(gates, 8, 7)
    rest = gates - first
    second = lax.reduce_precision(rest, 8, 7)
    third = rest - second
    return [part.astype(jnp.bfloat16) for part in (first, second, third)]


def block_rank(hits, tok_dev):
    grouped = hits.reshape(hits.shape[0], -1, tok_dev)
    earlier = jnp.arange(tok_dev)[:, None] > jnp.arange(tok_dev)[None, :]
    ranks = jnp.sum(jnp.where(earlier[None, None], grouped[:, :, None, :], 0), axis=-1)
    return ranks.reshape(hits.shape)


def per_device(tokens, upstream, expert_ids, gates, relocate, w_gate_up, w_down):
    n_rows = lax.axis_size("dp")
    n_cols = lax.axis_size("expert")
    slots = n_rows // SLICES
    experts = slots * n_cols
    tok_dev, width = tokens.shape
    top = expert_ids.shape[1]
    slice_width = w_down.shape[2]
    half = n_cols // 2
    col = lax.axis_index("expert")
    slot_here = lax.axis_index("dp") // SLICES
    y_groups = [[x * SLICES + y for y in range(SLICES)] for x in range(slots)]
    x_groups = [[x * SLICES + y for x in range(slots)] for y in range(SLICES)]

    own_pack = jnp.concatenate([w_gate_up[0, 0], w_down[0, 0]], axis=0)
    far_pack = half_swap(own_pack, n_cols, 0)

    meta = jnp.concatenate(
        [expert_ids.astype(jnp.bfloat16)] + three_parts(gates)
        + [jnp.zeros((tok_dev, 128 - 4 * top), jnp.bfloat16)],
        axis=1,
    )
    packed = jnp.concatenate([tokens, upstream, meta], axis=1)
    gathered = lax.all_gather(packed, "expert", axis=0, tiled=True)

    even = col % 2 == 0
    rel_row = jnp.sum(
        jnp.where(jnp.arange(n_cols)[:, None] == col, relocate, 0), axis=0
    )
    served = jnp.where(even, (col + half * rel_row) % n_cols, col) * slots + jnp.arange(slots)
    meta_all = gathered[:, 2 * width :].astype(jnp.float32)
    ids_all = meta_all[:, :top].astype(jnp.int32)
    gates_all = (
        meta_all[:, top : 2 * top] + meta_all[:, 2 * top : 3 * top] + meta_all[:, 3 * top : 4 * top]
    )
    match = ids_all[None] == served[:, None, None]
    hits = jnp.sum(match.astype(jnp.int32), axis=-1)
    gate_of = jnp.sum(jnp.where(match, gates_all[None], 0.0), axis=-1)
    n_tok = ids_all.shape[0]
    place = CAP * (jnp.arange(n_tok, dtype=jnp.int32) // tok_dev)[None] + block_rank(hits, tok_dev)
    seats = n_cols * CAP
    seat = (hits[:, None, :] > 0) & (
        place[:, None, :] == jnp.arange(seats, dtype=jnp.int32)[None, :, None]
    )
    select = seat.reshape(slots * seats, n_tok).astype(jnp.bfloat16)
    rows = jnp.dot(select, gathered[:, : 2 * width], preferred_element_type=jnp.float32)
    gate_rows = jnp.sum(jnp.where(seat, gate_of[:, None, :], 0.0), axis=-1).reshape(-1, 1)
    sent = jnp.concatenate(
        [rows[:, :width].astype(jnp.bfloat16), (gate_rows * rows[:, width:]).astype(jnp.bfloat16)], axis=1
    )

    at_x = lax.all_to_all(
        sent, "dp", split_axis=0, concat_axis=0, axis_index_groups=x_groups, tiled=True
    )
    all_rows = lax.all_gather(at_x, "dp", axis=0, axis_index_groups=y_groups, tiled=True)
    rows_x = all_rows[:, :width]
    rows_d = all_rows[:, width:]

    rel_here = jnp.sum(jnp.where(jnp.arange(slots) == slot_here, rel_row, 0))
    pack = jnp.where(even & (rel_here == 1), far_pack, own_pack)
    gate_up = pack[: 2 * slice_width]
    down_rows = pack[2 * slice_width :]
    gate_and_up = lax.dot_general(
        rows_x, gate_up, contract_last, preferred_element_type=jnp.float32
    )
    gate_pre = gate_and_up[:, :slice_width]
    up_pre = gate_and_up[:, slice_width:]
    activated, slope_of = silu_parts(gate_pre)
    hidden = (activated * up_pre).astype(jnp.bfloat16)
    hidden_grad = lax.dot_general(
        rows_d, down_rows, contract_last, preferred_element_type=jnp.float32
    )
    pre_grads = jnp.concatenate(
        [
            (hidden_grad * up_pre * slope_of).astype(jnp.bfloat16),
            (hidden_grad * activated).astype(jnp.bfloat16),
        ],
        axis=1,
    )
    slice_part = jnp.dot(pre_grads, gate_up, preferred_element_type=jnp.float32).astype(
        jnp.bfloat16
    )
    grad_gu = lax.dot_general(
        pre_grads, rows_x, contract_first, preferred_element_type=jnp.float32
    ).astype(jnp.bfloat16)
    grad_dn = lax.dot_general(
        hidden, rows_d, contract_first, preferred_element_type=jnp.float32
    ).astype(jnp.bfloat16)
    grad_pack = jnp.concatenate([grad_gu, grad_dn], axis=0)
    far_grads = half_swap(grad_pack, n_cols, 1)
    grad_pack = jnp.where(~even & (rel_here == 1), far_grads, grad_pack)

    parts = lax.all_to_all(
        slice_part, "dp", split_axis=0, concat_axis=0, axis_index_groups=y_groups, tiled=True
    )
    summed = jnp.sum(
        parts.reshape(SLICES, slots * seats, width).astype(jnp.float32), axis=0
    ).astype(jnp.bfloat16)
    back = lax.all_to_all(
        summed, "dp", split_axis=0, concat_axis=0, axis_index_groups=x_groups, tiled=True
    )
    partial = lax.dot_general(select, back, contract_first, preferred_element_type=jnp.float32)
    grad_tokens = lax.psum_scatter(
        partial, "expert", scatter_dimension=0, tiled=True
    ).astype(jnp.bfloat16)
    return (
        grad_tokens,
        grad_pack[: 2 * slice_width].reshape(w_gate_up.shape),
        grad_pack[2 * slice_width :].reshape(w_down.shape),
    )


def solution(mesh):
    return jax.shard_map(
        per_device,
        mesh=mesh,
        in_specs=(
            P(("dp", "expert"), None),
            P(("dp", "expert"), None),
            P(("dp", "expert"), None),
            P(("dp", "expert"), None),
            P(),
            P("expert", "dp", None, None),
            P("expert", "dp", None, None),
        ),
        out_specs=(
            P(("dp", "expert"), None),
            P("expert", "dp", None, None),
            P("expert", "dp", None, None),
        ),
        check_vma=False,
    )
```

time: 424 us -> 353 us (0.83)
  blocking collectives: 115 us -> 55.6 us
  waiting for transfers between devices: 206 us -> 241 us
  starting transfers between devices: 42.3 us -> 15.4 us
  other arithmetic: 26.9 us -> 5.47 us
  local copies, waits for them, and re-layouts: 20.2 us -> 7.03 us
  between operations: 1.76 us -> 14.7 us
    ppermute x5 -> x2, waiting for transfers between devices: 155 us -> 22.4 us  [half_swap(): return lax.ppermute(block, 'expert', route)]
    all_gather x0 -> x2, waiting for transfers between devices: none -> 126 us  [the longest x1 76 us: per_device(): gathered = lax.all_gather(packed, 'expert', axis=0, tiled=True)]
    reduce_scatter x0 -> x1, waiting for transfers between devices: none -> 92.7 us  [per_device(): lax.psum_scatter(partial, 'expert', scatter_dimension=0, tiled=True)]
    all_to_all x3, blocking collectives: 115 us -> 55.6 us  [the longest x1 24.1 us: per_device(): lax.all_to_all(slice_part, 'dp', split_axis=0, concat_axis=0, axis_index_...]
    all_to_all x1 -> x0, waiting for transfers between devices: 50.8 us -> none  [per_device(): lax.all_to_all(back_rows, 'expert', split_axis=1, concat_axis=1, tiled=True)]
    all_to_all x1 -> x0, starting transfers between devices: 26.5 us -> none  [per_device(): lax.all_to_all(back_rows, 'expert', split_axis=1, concat_axis=1, tiled=True)]
    concatenate x2 -> x3, other arithmetic: 10.7 us -> 0.25 us  [the longest x1 0.08 us: per_device(): own_pack = jnp.concatenate([w_gate_up[0, 0], w_down[0, 0]], axis=0)]
    select_n x5 -> x2, other arithmetic: 11.4 us -> 0.98 us  [the longest x1 0.5 us: per_device(): pack = jnp.where(even & (rel_here == 1), far_pack, own_pack)]
  transfers between devices with their start and end apart: 6 -> 5, of which waited for: 5 -> 4; matrix products, arithmetic and copies ran while one was open for 2% -> 2% of each run, Pallas kernels for 0% -> 0%
where the time goes in v1:
time: 353 us; the launch traced here: 352 us
  waiting for transfers between devices  241 us (68%)
  blocking collectives  55.6 us (16%)
  starting transfers between devices  15.4 us (4%)
  between operations  14.7 us (4%)
  matrix products  12.6 us (4%)
  local copies, waits for them, and re-layouts  7.03 us (2%)
  other arithmetic  5.47 us (2%)
    reduce_scatter x1, waiting for transfers between devices, per_device(): lax.psum_scatter(partial, 'expert', scatter_dimension=0, tiled=True)  92.7 us
    all_gather x1, waiting for transfers between devices, per_device(): gathered = lax.all_gather(packed, 'expert', axis=0, tiled=True)  76 us
    all_gather x1, waiting for transfers between devices, per_device(): lax.all_gather(at_x, 'dp', axis=0, axis_index_groups=y_groups, tiled=True)  49.8 us
    all_to_all x1, blocking collectives, per_device(): lax.all_to_all(slice_part, 'dp', split_axis=0, concat_axis=0, axis_index_...  24.1 us
    ppermute x2, waiting for transfers between devices, half_swap(): return lax.ppermute(block, 'expert', route)  22.4 us
    all_to_all x1, blocking collectives, per_device(): lax.all_to_all(sent, 'dp', split_axis=0, concat_axis=0, axis_index_groups...  18.6 us
    ppermute x2, starting transfers between devices, half_swap(): return lax.ppermute(block, 'expert', route)  15.3 us
    all_to_all x1, blocking collectives, per_device(): lax.all_to_all(summed, 'dp', split_axis=0, concat_axis=0, axis_index_grou...  12.8 us
  transfers between devices with their start and end apart: 5, of which 4 were waited for; matrix products, arithmetic and copies ran while one was open for 2% of the time, Pallas kernels for 0%

profile of v1, /device:TPU:1, one launch (start us, length us, event | category | flops | bytes accessed | tf_op | source)
XLA Modules:
  0.0 351.7 jit_solution(1204173419493060899)
XLA Ops:
  7.2 0.0 all-gather.3.cloned.1.call-start
  7.2 0.8 copy.30
  8.0 0.8 copy.31
  8.7 1.5 concatenate.15
  10.2 0.0 all-gather.3.cloned.1.call-update
  10.3 0.0 all-gather.5.cloned.1.call-start
  10.3 0.1 eq.76
  10.4 0.8 select_reduce_fusion.2
  11.2 0.6 iota_add_fusion
  11.9 76.0 %all-gather.3.cloned.1.call-done = bf16[512,2176]{1,0:T(8,128)(2,1)} async-done(((bf16[16,2176]{1,0:T(8,128)(2,1)}), bf16[512,2176]{1,0:T(8,128)(2,1)}) %all-gather.3.cloned.1.call-update) | async-done | bytes 2228240 | tf_op jit(solution)/shard_map/all_gather | solution.py:62
  87.8 0.9 slice.65
  88.8 0.1 copy.36
  88.9 0.1 fusion.27
  89.0 0.1 broadcast_in_dim.81
  89.1 0.1 fusion.28
  89.2 0.1 copy.34
  89.3 0.2 select_reduce_fusion.1
  89.5 0.1 copy.35
  89.6 0.1 reshape.106
  89.7 0.2 select_reduce_fusion
  89.9 0.1 mul.60
  90.0 0.2 fusion.22
  90.1 2.3 fusion
  92.4 0.1 slice.123
  92.5 0.1 fusion.16
  92.6 0.1 pad_maximum_fusion.2
  92.7 0.0 copy-start
  92.7 0.0 copy-start.1
  92.8 18.6 %all_to_all.30 = bf16[4,64,2048]{2,1,0:T(8,128)(2,1)} all-to-all(bf16[4,64,2048]{2,1,0:T(8,128)(2,1)S(1)} %bitcast.21), channel_id=1, replica_groups={{0,128,256,384},{32,160,288,416},{64,192,320,448},{96,224,352,480},{1,1..., dimensions={0} | all-to-all | bytes 2097152 | tf_op jit(solution)/shard_map/all_to_all | solution.py:90
  111.4 0.0 all-gather.5.cloned.1.call-update
  111.4 0.0 reduce-scatter.2.cloned.1.call-start
  111.5 0.0 copy-done
  111.5 0.0 copy-done.1
  111.5 0.1 pad_maximum_fusion
  111.6 0.7 collective-permute-start
  113.0 0.0 collective-permute-done
  113.0 0.5 broadcast_select_fusion.1
  113.5 49.8 %all-gather.5.cloned.1.call-done = bf16[1024,2048]{1,0:T(8,128)(2,1)} async-done(((bf16[256,2048]{1,0:T(8,128)(2,1)}), bf16[1024,2048]{1,0:T(8,128)(2,1)}) %all-gather.5.cloned.1.call-update) | async-done | bytes 4194320 | tf_op jit(solution)/shard_map/all_gather | solution.py:93
  163.3 0.0 copy-start.2
  163.3 2.7 fusion.4
  166.1 0.1 copy-done.2
  166.1 0.0 copy-start.4
  166.1 1.0 multiply_convert_fusion.2
  167.2 0.1 copy-done.4
  167.3 1.3 convolution_convert_fusion
  168.6 24.1 %all_to_all.31 = bf16[4,256,1024]{2,1,0:T(8,128)(2,1)S(1)} all-to-all(bf16[4,256,1024]{2,1,0:T(8,128)(2,1)S(1)} %bitcast.24), channel_id=1, replica_groups={{0,32,64,96},{128,160,192,224},{256,288,320,352},{384,416,448,480},{1,3..., dimensions={0} | all-to-all | bytes 4194304 | tf_op jit(solution)/shard_map/all_to_all | solution.py:131
  192.7 0.4 reduce_sum.72
  193.1 12.8 %all_to_all.32 = bf16[4,64,1024]{2,1,0:T(8,128)(2,1)S(1)} all-to-all(bf16[4,64,1024]{2,1,0:T(8,128)(2,1)S(1)} %bitcast.25), channel_id=1, replica_groups={{0,128,256,384},{32,160,288,416},{64,192,320,448},{96,224,352,480},{1,1..., dimensions={0} | all-to-all | bytes 1048576 | tf_op jit(solution)/shard_map/all_to_all | solution.py:137
  205.9 1.8 convolution_bitcast_fusion
  207.7 0.0 reduce-scatter.2.cloned.1.call-update
  207.8 0.0 copy-start.3
  207.8 0.0 copy-start.5
  207.8 2.7 fusion.10
  210.5 0.1 copy-done.3
  210.6 0.5 copy-done.5
  211.1 0.6 fusion.13
  211.7 0.1 pad_maximum_fusion.1
  211.8 14.6 %collective-permute-start.1 = (bf16[576,1024]{1,0:T(8,128)(2,1)S(1)}, bf16[576,1024]{1,0:T(8,128)(2,1)S(1)}, u32[]{:S(2)}, u32[]{:S(2)}) collective-permute-start(bf16[576,1024]{1,0:T(8,128)(2,1)S(1)} %pad_maximum_fusion.1), channel_id=1, source_target_pairs={{1,17},{3,19},{5,21},{7,23},{9,25},{11,27},{13,29},{15,31},{17,1},... | collective-permute-start | bytes 3538952 | tf_op jit(solution)/shard_map/ppermute | solution.py:21
  226.4 22.4 %collective-permute-done.1 = bf16[576,1024]{1,0:T(8,128)(2,1)S(1)} collective-permute-done((bf16[576,1024]{1,0:T(8,128)(2,1)S(1)}, bf16[576,1024]{1,0:T(8,128)(2,1)S(1)}, u32[]{:S(2)}, u32[]{:S(2)}) %collective-permute-start.1) | collective-permute-done | bytes 1179680 | tf_op jit(solution)/shard_map/ppermute | solution.py:21
  248.8 0.5 broadcast_select_fusion
  249.3 0.8 slice_bitcast_fusion.1
  250.1 0.9 slice_bitcast_fusion
  251.0 92.7 %reduce-scatter.2.cloned.1.call-done = f32[16,1024]{1,0:T(8,128)} async-done(((f32[512,1024]{1,0:T(8,128)}), f32[16,1024]{1,0:T(8,128)}) %reduce-scatter.2.cloned.1.call-update) | async-done | bytes 65552 | tf_op jit(solution)/shard_map/reduce_scatter | solution.py:141
  343.7 1.5 convert_element_type.60
  (11 shorter events, 0.1 us)
Async XLA Ops:
  7.2 80.7 %all-gather.3.cloned.1.call-start = ((), (), s32[]{:S(2)}) async-start(), calls=%async_computation.4 | async-start | bytes 2297856 | tf_op jit(solution)/shard_map/all_gather | solution.py:62
  10.3 153.1 %all-gather.5.cloned.1.call-start = ((), (), s32[]{:S(2)}) async-start(), calls=%async_computation.5 | async-start | bytes 5242880 | tf_op jit(solution)/shard_map/all_gather | solution.py:93
  92.7 18.7 %copy-start = (bf16[1,1,384,1024]{3,2,1,0:T(8,128)(2,1)S(1)}, bf16[1,1,384,1024]{3,2,1,0:T(8,128)(2,1)}, u32[]{:S(2)}) copy-start(bf16[1,1,384,1024]{3,2,1,0:T(8,128)(2,1)} %param.12) | copy-start | bytes 2359300
  92.7 18.7 %copy-start.1 = (bf16[1,1,192,1024]{3,2,1,0:T(8,128)(2,1)S(1)}, bf16[1,1,192,1024]{3,2,1,0:T(8,128)(2,1)}, u32[]{:S(2)}) copy-start(bf16[1,1,192,1024]{3,2,1,0:T(8,128)(2,1)} %param.13) | copy-start | bytes 1179652
  111.4 232.3 %reduce-scatter.2.cloned.1.call-start = ((), (), s32[]{:S(2)}) async-start(), calls=%async_computation.6 | async-start | bytes 2162688 | tf_op jit(solution)/shard_map/reduce_scatter | solution.py:141
  111.6 1.4 collective-permute-start
  163.3 2.8 copy-start.2
  166.1 1.1 copy-start.4
  207.8 2.8 copy-start.3
  207.8 3.3 copy-start.5
  211.8 37.0 %collective-permute-start.1 = (bf16[576,1024]{1,0:T(8,128)(2,1)S(1)}, bf16[576,1024]{1,0:T(8,128)(2,1)S(1)}, u32[]{:S(2)}, u32[]{:S(2)}) collective-permute-start(bf16[576,1024]{1,0:T(8,128)(2,1)S(1)} %pad_maximum_fusion.1), channel_id=1, source_target_pairs={{1,17},{3,19},{5,21},{7,23},{9,25},{11,27},{13,29},{15,31},{17,1},... | collective-permute-start | bytes 3538952 | tf_op jit(solution)/shard_map/ppermute | solution.py:21
Sparse Core Ops, SparseCore 0:
  10.7 77.1 all-gather.2
  111.5 51.7 all-gather.4
  207.9 135.8 reduce-scatter.1

commit v2 on v1

--- a/solution.py
+++ b/solution.py
@@ -1,13 +1,19 @@
+import functools
+
 import jax
 import jax.numpy as jnp
 from jax import lax
+from jax.experimental import pallas as pl
+from jax.experimental.pallas import tpu as pltpu
 from jax.sharding import PartitionSpec as P
 
 SLICES = 4
 CAP = 2
+MESH = pl.DeviceIdType.MESH
 
 contract_last = (((1,), (1,)), ((), ()))
 contract_first = (((0,), (0,)), ((), ()))
+VMEM_SPEC = pl.BlockSpec(memory_space=pltpu.VMEM)
 
 
 def silu_parts(values_in):
@@ -36,22 +42,329 @@
     return ranks.reshape(hits.shape)
 
 
+def meet(peers):
+    barrier = pltpu.get_barrier_semaphore()
+    for peer in peers:
+        pl.semaphore_signal(barrier, inc=1, device_id=peer, device_id_type=MESH)
+    pl.semaphore_wait(barrier, len(peers))
+
+
+def remote(src, dst, send_sem, recv_sem, peer):
+    return pltpu.make_async_remote_copy(
+        src_ref=src, dst_ref=dst, send_sem=send_sem, recv_sem=recv_sem,
+        device_id=peer, device_id_type=MESH,
+    )
+
+
+def gather_kernel(n_cols, own_ref, all_ref, keep_sem, send_p, recv_p, send_m, recv_m, send_s, recv_s):
+    e = lax.axis_index("expert")
+    chips = n_cols // 2
+    ahead = {"expert": lax.rem(e + 2, n_cols)}
+    behind = {"expert": lax.rem(e + n_cols - 2, n_cols)}
+    twin = {"expert": e + 1 - 2 * lax.rem(e, 2)}
+    meet([ahead, behind, twin])
+    up_steps, down_steps = chips // 2, chips // 2 - 1
+    parts = own_ref.shape[0]
+
+    def slot(shift, h):
+        return parts * lax.rem(e + 2 * shift + n_cols, n_cols) + h
+
+    def up(s, h, src):
+        return remote(src, all_ref.at[slot(-s, h)], send_p.at[s, h], recv_p.at[s, h], ahead)
+
+    def down(s, h, src):
+        return remote(src, all_ref.at[slot(s, h)], send_m.at[s, h], recv_m.at[s, h], behind)
+
+    def side(shift, h, src):
+        index = shift % chips
+        return remote(src, all_ref.at[slot(shift, h)], send_s.at[index, h], recv_s.at[index, h], twin)
+
+    started = []
+    keeps = []
+    for h in range(parts):
+        for copy in (up(0, h, own_ref.at[h]), down(0, h, own_ref.at[h]), side(0, h, own_ref.at[h])):
+            copy.start()
+            started.append(copy)
+        keep = pltpu.make_async_copy(own_ref.at[h], all_ref.at[slot(0, h)], keep_sem.at[h])
+        keep.start()
+        keeps.append(keep)
+    for s in range(1, up_steps + 1):
+        for h in range(parts):
+            block = all_ref.at[slot(-s, h)]
+            up(s - 1, h, block).wait_recv()
+            if s < up_steps:
+                copy = up(s, h, block)
+                copy.start()
+                started.append(copy)
+            copy = side(-s, h, block)
+            copy.start()
+            started.append(copy)
+            if s <= down_steps:
+                block = all_ref.at[slot(s, h)]
+                down(s - 1, h, block).wait_recv()
+                if s < down_steps:
+                    copy = down(s, h, block)
+                    copy.start()
+                    started.append(copy)
+                copy = side(s, h, block)
+                copy.start()
+                started.append(copy)
+    for shift in range(-up_steps, down_steps + 1):
+        for h in range(parts):
+            other = parts * lax.rem(e + 1 - 2 * lax.rem(e, 2) + 2 * shift + n_cols, n_cols) + h
+            index = shift % chips
+            remote(all_ref.at[other], all_ref.at[other], send_s.at[index, h], recv_s.at[index, h], twin).wait_recv()
+    for copy in started:
+        copy.wait_send()
+    for keep in keeps:
+        keep.wait()
+
+
+def gather_tokens(packed, n_cols):
+    parts, rows, width = packed.shape
+    chips = n_cols // 2
+    up, down = chips // 2, chips // 2 - 1
+    dma = pltpu.SemaphoreType.DMA
+    return pl.pallas_call(
+        functools.partial(gather_kernel, n_cols),
+        out_shape=jax.ShapeDtypeStruct((n_cols * parts, rows, width), packed.dtype),
+        in_specs=[VMEM_SPEC],
+        out_specs=VMEM_SPEC,
+        scratch_shapes=[
+            dma((parts,)), dma((up, parts)), dma((up, parts)), dma((down, parts)), dma((down, parts)),
+            dma((chips, parts)), dma((chips, parts)),
+        ],
+        compiler_params=pltpu.CompilerParams(collective_id=0, has_side_effects=True),
+        name="gather_tokens",
+    )(packed)
+
+
+def xy_peers():
+    row = lax.axis_index("dp")
+    my_x, my_y = row // SLICES, lax.rem(row, SLICES)
+
+    def at(dx, dy):
+        return {"dp": lax.rem(my_x + dx, SLICES) * SLICES + lax.rem(my_y + dy, SLICES)}
+
+    return my_x, my_y, at
+
+
+def dispatch_kernel(sent_ref, all_ref, keep_sem, send_x, recv_x, send_y, recv_y, send_f, recv_f):
+    my_x, my_y, at = xy_peers()
+    north, south = at(0, 1), at(0, 3)
+    meet([at(1, 0), at(2, 0), at(3, 0), north, south])
+    half = sent_ref.shape[1] // 2
+    low, high = pl.ds(0, half), pl.ds(half, half)
+    x_of = [lax.rem(my_x + k, SLICES) for k in range(SLICES)]
+    y_of = [lax.rem(my_y + k, SLICES) for k in range(SLICES)]
+    started = []
+
+    def go(copy):
+        copy.start()
+        started.append(copy)
+
+    keep = pltpu.make_async_copy(sent_ref.at[my_x], all_ref.at[my_y, my_x], keep_sem)
+    keep.start()
+
+    def x_copy(k):
+        return remote(
+            sent_ref.at[x_of[k]], all_ref.at[my_y, my_x], send_x.at[SLICES - k], recv_x.at[SLICES - k], at(k, 0)
+        )
+
+    def y_send(k, src):
+        block = all_ref.at[my_y, x_of[k]]
+        go(remote(src, block, send_y.at[0, k], recv_y.at[0, k], north))
+        go(remote(src, block, send_y.at[1, k], recv_y.at[1, k], south))
+
+    def x_then_y(k):
+        block = all_ref.at[my_y, x_of[k]]
+        remote(block, block, send_x.at[k], recv_x.at[k], at(k, 0)).wait_recv()
+        y_send(k, block)
+
+    def pass_on(k):
+        block = all_ref.at[y_of[3], x_of[k]]
+        remote(block, block, send_y.at[0, k], recv_y.at[0, k], south).wait_recv()
+        part = all_ref.at[y_of[3], x_of[k], low]
+        go(remote(part, part, send_f.at[0, k], recv_f.at[0, k], north))
+        block = all_ref.at[y_of[1], x_of[k]]
+        remote(block, block, send_y.at[1, k], recv_y.at[1, k], north).wait_recv()
+        part = all_ref.at[y_of[1], x_of[k], high]
+        go(remote(part, part, send_f.at[1, k], recv_f.at[1, k], south))
+
+    y_send(0, sent_ref.at[my_x])
+    for k in (1, 3, 2):
+        go(x_copy(k))
+    x_then_y(1)
+    x_then_y(3)
+    pass_on(0)
+    x_then_y(2)
+    pass_on(1)
+    pass_on(3)
+    pass_on(2)
+    for k in range(SLICES):
+        part = all_ref.at[y_of[2], x_of[k], low]
+        remote(part, part, send_f.at[0, k], recv_f.at[0, k], south).wait_recv()
+        part = all_ref.at[y_of[2], x_of[k], high]
+        remote(part, part, send_f.at[1, k], recv_f.at[1, k], north).wait_recv()
+    for copy in started:
+        copy.wait_send()
+    keep.wait()
+
+
+def dispatch_rows(sent):
+    slots, seats, width = sent.shape
+    dma = pltpu.SemaphoreType.DMA
+    return pl.pallas_call(
+        dispatch_kernel,
+        out_shape=jax.ShapeDtypeStruct((SLICES, slots, seats, width), sent.dtype),
+        in_specs=[VMEM_SPEC],
+        out_specs=VMEM_SPEC,
+        scratch_shapes=[
+            dma, dma((SLICES,)), dma((SLICES,)), dma((2, SLICES)), dma((2, SLICES)), dma((2, SLICES)), dma((2, SLICES)),
+        ],
+        compiler_params=pltpu.CompilerParams(collective_id=1, has_side_effects=True),
+        cost_estimate=pl.CostEstimate(flops=0, bytes_accessed=150_000_000, transcendentals=0),
+        name="dispatch_rows",
+    )(sent)
+
+
+def return_kernel(
+    part_ref, back_ref, relay, summed, got, total,
+    send_r, recv_r, send_d, recv_d, send_t, recv_t, send_x, recv_x, keep_sem,
+):
+    my_x, my_y, at = xy_peers()
+    north, south = at(0, 1), at(0, 3)
+    meet([at(1, 0), at(2, 0), at(3, 0), north, south])
+    y_of = [lax.rem(my_y + k, SLICES) for k in range(SLICES)]
+    pair = SLICES // 2
+    started = []
+
+    def go(copy):
+        copy.start()
+        started.append(copy)
+
+    def relay_copy(way, i):
+        block = pair * (1 - way) + i
+        return remote(
+            part_ref.at[y_of[2], block], relay.at[way, i], send_r.at[way, i], recv_r.at[way, i], (north, south)[way]
+        )
+
+    def direct_copy(way, i):
+        block = pair * way + i
+        return remote(
+            part_ref.at[y_of[1 if way == 0 else 3], block], got.at[way, block],
+            send_d.at[way, i], recv_d.at[way, i], (north, south)[way],
+        )
+
+    def total_copy(way, i):
+        block = pair * (1 - way) + i
+        return remote(
+            summed.at[way, i], got.at[way, block], send_t.at[way, i], recv_t.at[way, i], (north, south)[way]
+        )
+
+    for i in range(pair):
+        for way in range(2):
+            go(relay_copy(way, i))
+    for i in range(pair):
+        for way in range(2):
+            go(direct_copy(way, i))
+    for i in range(pair):
+        for way in range(2):
+            relay_copy(way, i).wait_recv()
+            block = pair * (1 - way) + i
+            mine = part_ref[y_of[1 if way == 0 else 3], block].astype(jnp.float32)
+            summed[way, i] = (mine + relay[way, i].astype(jnp.float32)).astype(jnp.bfloat16)
+            go(total_copy(way, i))
+    for i in range(pair):
+        for way in range(2):
+            direct_copy(way, i).wait_recv()
+            total_copy(way, i).wait_recv()
+    for k in (2, 1, 3, 0):
+        block = lax.rem(my_x + k, SLICES)
+        total[block] = (
+            part_ref[my_y, block].astype(jnp.float32)
+            + got[0, block].astype(jnp.float32)
+            + got[1, block].astype(jnp.float32)
+        ).astype(jnp.bfloat16)
+        if k > 0:
+            go(remote(
+                total.at[block], back_ref.at[my_x], send_x.at[SLICES - k], recv_x.at[SLICES - k], at(k, 0)
+            ))
+        else:
+            keep = pltpu.make_async_copy(total.at[block], back_ref.at[my_x], keep_sem)
+            keep.start()
+            keep.wait()
+    for k in (1, 3, 2):
+        block = back_ref.at[lax.rem(my_x + k, SLICES)]
+        remote(block, block, send_x.at[k], recv_x.at[k], at(k, 0)).wait_recv()
+    for copy in started:
+        copy.wait_send()
+
+
+def return_rows(parts):
+    _, slots, seats, width = parts.shape
+    dma = pltpu.SemaphoreType.DMA
+    pair = SLICES // 2
+    return pl.pallas_call(
+        return_kernel,
+        out_shape=jax.ShapeDtypeStruct((slots, seats, width), parts.dtype),
+        in_specs=[VMEM_SPEC],
+        out_specs=VMEM_SPEC,
+        scratch_shapes=[
+            pltpu.VMEM((2, pair, seats, width), jnp.bfloat16),
+            pltpu.VMEM((2, pair, seats, width), jnp.bfloat16),
+            pltpu.VMEM((2, slots, seats, width), jnp.bfloat16),
+            pltpu.VMEM((slots, seats, width), jnp.bfloat16),
+        ] + [dma((2, pair))] * 6 + [dma((SLICES,))] * 2 + [dma],
+        compiler_params=pltpu.CompilerParams(collective_id=2, has_side_effects=True),
+        cost_estimate=pl.CostEstimate(flops=0, bytes_accessed=100_000_000, transcendentals=0),
+        name="return_rows",
+    )(parts)
+
+
+def home_kernel(n_cols, rows_ref, home_ref, send_sem, recv_sem, keep_sem):
+    e = lax.axis_index("expert")
+    peers = [{"expert": lax.rem(e + k, n_cols)} for k in range(n_cols)]
+    meet(peers[1:])
+    order = sorted(range(1, n_cols), key=lambda k: -min(k, n_cols - k))
+    for k in order:
+        remote(
+            rows_ref.at[lax.rem(e + k, n_cols)], home_ref.at[e], send_sem.at[k], recv_sem.at[k], peers[k]
+        ).start()
+    keep = pltpu.make_async_copy(rows_ref.at[e], home_ref.at[e], keep_sem)
+    keep.start()
+    keep.wait()
+    for k in order:
+        block = home_ref.at[lax.rem(e + n_cols - k, n_cols)]
+        remote(block, block, send_sem.at[k], recv_sem.at[k], peers[k]).wait()
+
+
+def bring_home(rows):
+    n_cols = rows.shape[0]
+    dma = pltpu.SemaphoreType.DMA
+    return pl.pallas_call(
+        functools.partial(home_kernel, n_cols),
+        out_shape=jax.ShapeDtypeStruct(rows.shape, rows.dtype),
+        in_specs=[VMEM_SPEC],
+        out_specs=VMEM_SPEC,
+        scratch_shapes=[dma((n_cols,)), dma((n_cols,)), dma],
+        compiler_params=pltpu.CompilerParams(collective_id=3, has_side_effects=True),
+        cost_estimate=pl.CostEstimate(flops=0, bytes_accessed=100_000_000, transcendentals=0),
+        name="bring_home",
+    )(rows)
+
+
 def per_device(tokens, upstream, expert_ids, gates, relocate, w_gate_up, w_down):
     n_rows = lax.axis_size("dp")
     n_cols = lax.axis_size("expert")
     slots = n_rows // SLICES
-    experts = slots * n_cols
     tok_dev, width = tokens.shape
     top = expert_ids.shape[1]
     slice_width = w_down.shape[2]
     half = n_cols // 2
+    seats = n_cols * CAP
     col = lax.axis_index("expert")
     slot_here = lax.axis_index("dp") // SLICES
-    y_groups = [[x * SLICES + y for y in range(SLICES)] for x in range(slots)]
-    x_groups = [[x * SLICES + y for x in range(slots)] for y in range(SLICES)]
-
-    own_pack = jnp.concatenate([w_gate_up[0, 0], w_down[0, 0]], axis=0)
-    far_pack = half_swap(own_pack, n_cols, 0)
 
     meta = jnp.concatenate(
         [expert_ids.astype(jnp.bfloat16)] + three_parts(gates)
@@ -59,7 +372,12 @@
         axis=1,
     )
     packed = jnp.concatenate([tokens, upstream, meta], axis=1)
-    gathered = lax.all_gather(packed, "expert", axis=0, tiled=True)
+    gathered = gather_tokens(packed.reshape(2, tok_dev // 2, -1), n_cols)
+
+    own_pack = jnp.concatenate([w_gate_up[0, 0], w_down[0, 0]], axis=0)
+    gathered, own_pack = lax.optimization_barrier((gathered, own_pack))
+    far_pack = half_swap(own_pack, n_cols, 0)
+    gathered = gathered.reshape(n_cols * tok_dev, -1)
 
     even = col % 2 == 0
     rel_row = jnp.sum(
@@ -76,7 +394,6 @@
     gate_of = jnp.sum(jnp.where(match, gates_all[None], 0.0), axis=-1)
     n_tok = ids_all.shape[0]
     place = CAP * (jnp.arange(n_tok, dtype=jnp.int32) // tok_dev)[None] + block_rank(hits, tok_dev)
-    seats = n_cols * CAP
     seat = (hits[:, None, :] > 0) & (
         place[:, None, :] == jnp.arange(seats, dtype=jnp.int32)[None, :, None]
     )
@@ -87,10 +404,7 @@
         [rows[:, :width].astype(jnp.bfloat16), (gate_rows * rows[:, width:]).astype(jnp.bfloat16)], axis=1
     )
 
-    at_x = lax.all_to_all(
-        sent, "dp", split_axis=0, concat_axis=0, axis_index_groups=x_groups, tiled=True
-    )
-    all_rows = lax.all_gather(at_x, "dp", axis=0, axis_index_groups=y_groups, tiled=True)
+    all_rows = dispatch_rows(sent.reshape(slots, seats, 2 * width)).reshape(-1, 2 * width)
     rows_x = all_rows[:, :width]
     rows_d = all_rows[:, width:]
 
@@ -125,22 +439,32 @@
         hidden, rows_d, contract_first, preferred_element_type=jnp.float32
     ).astype(jnp.bfloat16)
     grad_pack = jnp.concatenate([grad_gu, grad_dn], axis=0)
+    slice_part, grad_pack = lax.optimization_barrier((slice_part, grad_pack))
     far_grads = half_swap(grad_pack, n_cols, 1)
     grad_pack = jnp.where(~even & (rel_here == 1), far_grads, grad_pack)
 
-    parts = lax.all_to_all(
-        slice_part, "dp", split_axis=0, concat_axis=0, axis_index_groups=y_groups, tiled=True
-    )
-    summed = jnp.sum(
-        parts.reshape(SLICES, slots * seats, width).astype(jnp.float32), axis=0
-    ).astype(jnp.bfloat16)
-    back = lax.all_to_all(
-        summed, "dp", split_axis=0, concat_axis=0, axis_index_groups=x_groups, tiled=True
-    )
-    partial = lax.dot_general(select, back, contract_first, preferred_element_type=jnp.float32)
-    grad_tokens = lax.psum_scatter(
-        partial, "expert", scatter_dimension=0, tiled=True
-    ).astype(jnp.bfloat16)
+    back = return_rows(slice_part.reshape(SLICES, slots, seats, width))
+    rows_home = (
+        back.reshape(slots, n_cols, CAP, width).transpose(1, 0, 2, 3).reshape(n_cols, slots * CAP, width)
+    )
+    home = bring_home(rows_home).reshape(n_cols * slots * CAP, width)
+
+    flat_ids = expert_ids.reshape(-1)
+    experts = slots * n_cols
+    relocated = jnp.sum(
+        jnp.where(flat_ids[:, None] == jnp.arange(experts)[None, :], relocate.reshape(1, experts), 0), axis=1
+    )
+    home_col = flat_ids // slots
+    served_col = jnp.where(home_col % 2 == 0, (home_col + half * relocated) % n_cols, home_col)
+    token_of = jnp.arange(flat_ids.shape[0], dtype=jnp.int32) // top
+    earlier = (flat_ids[:, None] == flat_ids[None, :]) & (token_of[None, :] < token_of[:, None])
+    rank = jnp.sum(earlier.astype(jnp.int32), axis=1)
+    target = ((served_col * slots + flat_ids % slots) * CAP + rank).reshape(tok_dev, top)
+    picks = jnp.sum(
+        (target[:, :, None] == jnp.arange(home.shape[0], dtype=jnp.int32)[None, None, :]).astype(jnp.bfloat16),
+        axis=1,
+    )
+    grad_tokens = jnp.dot(picks, home, preferred_element_type=jnp.float32).astype(jnp.bfloat16)
     return (
         grad_tokens,
         grad_pack[: 2 * slice_width].reshape(w_gate_up.shape),

time: 353 us -> 201 us (0.57)
  waiting for transfers between devices: 241 us -> 0.01 us
  Pallas kernels: 0 us -> 159 us
  blocking collectives: 55.6 us -> 0 us
  between operations: 14.7 us -> 1.57 us
  starting transfers between devices: 15.4 us -> 8.6 us
  other arithmetic: 5.47 us -> 10.2 us
    pallas_call x0 -> x4, Pallas kernels: none -> 159 us  [the longest x1 42.6 us: bring_home(): pl.pallas_call(functools.partial(home_kernel, n_cols), out_shape=jax.Shap...]
    all_gather x2 -> x0, waiting for transfers between devices: 126 us -> none  [the longest x1 76 us: per_device(): gathered = lax.all_gather(packed, 'expert', axis=0, tiled=True)]
    reduce_scatter x1 -> x0, waiting for transfers between devices: 92.7 us -> none  [per_device(): lax.psum_scatter(partial, 'expert', scatter_dimension=0, tiled=True)]
    all_to_all x3 -> x0, blocking collectives: 55.6 us -> none  [the longest x1 24.1 us: per_device(): lax.all_to_all(slice_part, 'dp', split_axis=0, concat_axis=0, axis_index_...]
    ppermute x2, waiting for transfers between devices: 22.4 us -> 0.01 us  [half_swap(): return lax.ppermute(block, 'expert', route)]
    ppermute x2, starting transfers between devices: 15.3 us -> 8.6 us  [half_swap(): return lax.ppermute(block, 'expert', route)]
  transfers between devices with their start and end apart: 5 -> 2, of which waited for: 4 -> 0; matrix products, arithmetic and copies ran while one was open for 2% -> 8% of each run, Pallas kernels for 0% -> 58%
where the time goes in v2:
time: 201 us; the launch traced here: 200 us
  Pallas kernels  159 us (79%)
  matrix products  10.7 us (5%)
  other arithmetic  10.2 us (5%)
  local copies, waits for them, and re-layouts  9.74 us (5%)
  starting transfers between devices  8.6 us (4%)
    pallas_call x1, Pallas kernels, bring_home(): pl.pallas_call(functools.partial(home_kernel, n_cols), out_shape=jax.Shap...  42.6 us
    pallas_call x1, Pallas kernels, gather_tokens(): pl.pallas_call(functools.partial(gather_kernel, n_cols), out_shape=jax.Sh...  42.3 us
    pallas_call x1, Pallas kernels, dispatch_rows(): pl.pallas_call(dispatch_kernel, out_shape=jax.ShapeDtypeStruct((SLICES, s...  42.1 us
    pallas_call x1, Pallas kernels, return_rows(): pl.pallas_call(return_kernel, out_shape=jax.ShapeDtypeStruct((slots, seat...  32.4 us
    ppermute x2, starting transfers between devices, half_swap(): return lax.ppermute(block, 'expert', route)  8.6 us
  transfers between devices with their start and end apart: 2, of which 0 were waited for; matrix products, arithmetic and copies ran while one was open for 8% of the time, Pallas kernels for 58%

profile of v2, /device:TPU:1, one launch (start us, length us, event | category | flops | bytes accessed | tf_op | source)
XLA Modules:
  0.0 200.1 jit_solution(5303405490524282615)
XLA Ops:
  0.6 0.7 convert_element_type.57
  1.3 0.1 copy.53
  1.4 0.7 fusion.39
  2.1 0.1 copy.56
  2.2 0.1 copy.55
  2.3 0.1 copy.54
  2.4 1.5 concatenate.15
  3.9 42.3 %gather_tokens.1 = bf16[64,8,2176]{2,1,0:T(8,128)(2,1)} custom-call(bf16[2,8,2176]{2,1,0:T(8,128)(2,1)} %bitcast.36), custom_call_target="tpu_custom_call" | custom-call | tf_op jit(solution)/shard_map/gather_tokens/pallas_call | solution.py:128
  46.1 0.0 copy-start.3
  46.1 1.5 pad_maximum_fusion
  47.6 1.7 collective-permute-start
  49.3 0.6 fusion.40
  49.9 0.6 iota_compare_fusion.3
  50.5 0.1 select_reduce_fusion.3
  50.6 0.6 iota_add_fusion
  51.9 0.7 eq.133
  52.6 0.0 copy-done
  52.6 0.7 slice.65
  53.3 1.0 copy.61
  54.3 0.1 fusion.26
  54.4 0.0 copy-done.5
  54.4 0.8 fusion.27
  55.2 0.1 broadcast_in_dim.102
  55.3 0.1 copy.58
  55.3 0.9 select_reduce_fusion.1
  56.2 0.1 copy.59
  56.3 0.1 reshape.219
  56.4 0.7 broadcast_add_fusion
  57.1 0.2 select_reduce_fusion
  57.3 0.1 mul.88
  57.4 0.8 fusion.22
  58.2 0.7 fusion
  58.9 0.1 slice.123
  59.0 0.1 fusion.16
  59.1 1.1 pad_maximum_fusion.2
  60.2 42.1 %dispatch_rows.1 = bf16[4,4,64,2048]{3,2,1,0:T(8,128)(2,1)} custom-call(bf16[4,64,2048]{2,1,0:T(8,128)(2,1)} %bitcast.31), custom_call_target="tpu_custom_call" | custom-call | bytes 150000000 | tf_op jit(solution)/shard_map/dispatch_rows/pallas_call | solution.py:217
  102.3 0.0 collective-permute-done
  102.3 0.1 broadcast_select_fusion.1
  102.5 2.8 %fusion.4 = f32[1024,384]{0,1:T(8,128)S(1)} fusion(bf16[1024,2048]{1,0:T(8,128)(2,1)} %bitcast.27, bf16[576,1024]{1,0:T(8,128)(2,1)S(1)} %broadcast_select_fusion.1), kind=kOutput, calls=%fused_computation.5 | convolution fusion | flops 805306368 | bytes 4456448 | tf_op jit(solution)/shard_map/dot_general | solution.py:415
  105.2 0.1 copy-done.1
  105.3 0.7 fusion.13
  106.0 1.0 multiply_convert_fusion.2
  107.0 1.0 fusion.10
  108.0 2.6 %convolution_convert_fusion = bf16[1024,1024]{1,0:T(8,128)(2,1)} fusion(bf16[576,1024]{1,0:T(8,128)(2,1)S(1)} %broadcast_select_fusion.1, bf16[1024,192]{0,1:T(8,128)(2,1)S(1)} %get-tuple-element.14, bf16[1024,192]{0,1:T(8,128)(2,1)S(1)} %get-tuple-element.13), kind=kOutput, calls=%fused_computation.2 | convolution fusion | flops 807927808 | bytes 3670016 | tf_op jit(solution)/shard_map/dot_general | solution.py:432
  110.7 0.1 pad_maximum_fusion.1
  110.7 6.9 %collective-permute-start.1 = (bf16[576,1024]{1,0:T(8,128)(2,1)S(1)}, bf16[576,1024]{1,0:T(8,128)(2,1)S(1)}, u32[]{:S(2)}, u32[]{:S(2)}) collective-permute-start(bf16[576,1024]{1,0:T(8,128)(2,1)S(1)} %pad_maximum_fusion.1), channel_id=1, source_target_pairs={{1,17},{3,19},{5,21},{7,23},{9,25},{11,27},{13,29},{15,31},{17,1},... | collective-permute-start | bytes 3538952 | tf_op jit(solution)/shard_map/ppermute | solution.py:27
  117.7 0.1 copy.47
  117.8 0.1 copy.52
  117.9 0.1 eq.115
  117.9 0.1 broadcast_in_dim.95
  118.1 0.2 select_reduce_fusion.2
  118.2 0.1 mul.81
  118.3 0.1 reduce_sum.88
  118.5 0.1 fusion.28
  118.6 32.4 %return_rows.1 = bf16[4,64,1024]{2,1,0:T(8,128)(2,1)} custom-call(bf16[4,4,64,1024]{3,2,1,0:T(8,128)(2,1)} %bitcast.32), custom_call_target="tpu_custom_call" | custom-call | bytes 100000000 | tf_op jit(solution)/shard_map/return_rows/pallas_call | solution.py:308
  151.0 1.2 reshape.223
  152.2 0.5 copy.63
  152.7 1.0 reshape.224.rows_ref
  153.7 42.6 %bring_home.1 = bf16[32,8,1024]{2,1,0:T(8,128)(2,1)} custom-call(bf16[32,8,1024]{2,1,0:T(8,128)(2,1)} %reshape.224.rows_ref), custom_call_target="tpu_custom_call" | custom-call | bytes 100000000 | tf_op jit(solution)/shard_map/bring_home/pallas_call | solution.py:345
  196.4 1.8 convolution_convert_fusion.1
  198.2 0.0 collective-permute-done.1
  198.2 0.1 broadcast_select_fusion
  198.4 0.8 slice_bitcast_fusion.1
  199.1 0.9 slice_bitcast_fusion
  (17 shorter events, 0.1 us)
Async XLA Ops:
  46.1 4.4 %copy-start.3 = (s32[32,4]{0,1:T(4,128)S(1)}, s32[32,4]{0,1:T(4,128)}, u32[]{:S(2)}) copy-start(s32[32,4]{0,1:T(4,128)} %param.11) | copy-start | bytes 1540
  46.1 6.4 %copy-start = (bf16[64,8,2176]{2,1,0:T(8,128)(2,1)S(1)}, bf16[64,8,2176]{2,1,0:T(8,128)(2,1)}, u32[]{:S(2)}) copy-start(bf16[64,8,2176]{2,1,0:T(8,128)(2,1)} %gather_tokens.1) | copy-start | bytes 6684676
  47.6 54.7 %collective-permute-start = (bf16[576,1024]{1,0:T(8,128)(2,1)S(1)}, bf16[576,1024]{1,0:T(8,128)(2,1)}, u32[]{:S(2)}, u32[]{:S(2)}) collective-permute-start(bf16[576,1024]{1,0:T(8,128)(2,1)S(1)} %pad_maximum_fusion), channel_id=1, source_target_pairs={{0,16},{2,18},{4,20},{6,22},{8,24},{10,26},{12,28},{14,30},{16,0},... | collective-permute-start | bytes 3538952 | tf_op jit(solution)/shard_map/ppermute | solution.py:27
  51.2 3.2 %copy-start.5 = (s32[4]{0:T(128)}, s32[4]{0:T(128)S(1)}, u32[]{:S(2)}) copy-start(s32[4]{0:T(128)S(1)} %get-tuple-element.20) | copy-start | bytes 52
  102.5 2.8 %copy-start.1 = (bf16[4,4,64,2048]{3,2,1,0:T(8,128)(2,1)S(1)}, bf16[4,4,64,2048]{3,2,1,0:T(8,128)(2,1)}, u32[]{:S(2)}) copy-start(bf16[4,4,64,2048]{3,2,1,0:T(8,128)(2,1)} %dispatch_rows.1) | copy-start | bytes 12582916
  110.7 7.0 %copy-start.2 = (s32[16,8]{0,1:T(8,128)S(1)}, s32[16,8]{0,1:T(8,128)}, u32[]{:S(2)}) copy-start(s32[16,8]{0,1:T(8,128)} %param.9) | copy-start | bytes 1540
  110.7 7.1 %copy-start.4 = (s32[32,4]{0,1:T(4,128)S(1)}, s32[32,4]{0,1:T(4,128)}, u32[]{:S(2)}) copy-start(s32[32,4]{0,1:T(4,128)} %param.11) | copy-start | bytes 1540
  110.7 87.5 %collective-permute-start.1 = (bf16[576,1024]{1,0:T(8,128)(2,1)S(1)}, bf16[576,1024]{1,0:T(8,128)(2,1)S(1)}, u32[]{:S(2)}, u32[]{:S(2)}) collective-permute-start(bf16[576,1024]{1,0:T(8,128)(2,1)S(1)} %pad_maximum_fusion.1), channel_id=1, source_target_pairs={{1,17},{3,19},{5,21},{7,23},{9,25},{11,27},{13,29},{15,31},{17,1},... | collective-permute-start | bytes 3538952 | tf_op jit(solution)/shard_map/ppermute | solution.py:27

commit v3 on v2

v3 whole, which is shorter than its diff:
```python
import functools

import jax
import jax.numpy as jnp
from jax import lax
from jax.experimental import pallas as pl
from jax.experimental.pallas import tpu as pltpu
from jax.sharding import PartitionSpec as P

SLICES = 4
CAP = 2
MESH = pl.DeviceIdType.MESH

contract_last = (((1,), (1,)), ((), ()))
contract_first = (((0,), (0,)), ((), ()))
VMEM_SPEC = pl.BlockSpec(memory_space=pltpu.VMEM)


def silu_parts(values_in):
    sigmoid_of = jax.nn.sigmoid(values_in)
    return (values_in * sigmoid_of, sigmoid_of * (1.0 + values_in * (1.0 - sigmoid_of)))


def half_swap(block, count, parity):
    half = count // 2
    route = [(c, (c + half) % count) for c in range(count) if c % 2 == parity]
    return lax.ppermute(block, "expert", route)


def three_parts(gates):
    first = lax.reduce_precision(gates, 8, 7)
    rest = gates - first
    second = lax.reduce_precision(rest, 8, 7)
    third = rest - second
    return [part.astype(jnp.bfloat16) for part in (first, second, third)]


def meet(peers):
    barrier = pltpu.get_barrier_semaphore()
    for peer in peers:
        pl.semaphore_signal(barrier, inc=1, device_id=peer, device_id_type=MESH)
    pl.semaphore_wait(barrier, len(peers))


def remote(src, dst, send_sem, recv_sem, peer):
    return pltpu.make_async_remote_copy(
        src_ref=src, dst_ref=dst, send_sem=send_sem, recv_sem=recv_sem,
        device_id=peer, device_id_type=MESH,
    )


def xy_peers():
    row = lax.axis_index("dp")
    my_x, my_y = row // SLICES, lax.rem(row, SLICES)

    def at(dx, dy):
        return {"dp": lax.rem(my_x + dx, SLICES) * SLICES + lax.rem(my_y + dy, SLICES)}

    return my_x, my_y, at


def near_order(chips):
    order = [0]
    for s in range(1, chips // 2):
        order += [s, -s]
    return order + [-(chips // 2)]


def pick_rows(block, lane_ids, row_ids, tok_dev, seats):
    n_tok, width = block.shape[0], (block.shape[1] - 128) // 2
    top = 8
    meta = block[:, 2 * width :].astype(jnp.float32)
    hit = meta[:, 0:1] == lane_ids
    for k in range(1, top):
        hit = hit | (meta[:, k : k + 1] == lane_ids)
    hits = jnp.where(hit, 1.0, 0.0)
    t_row = lax.broadcasted_iota(jnp.int32, (n_tok, n_tok), 0)
    t_col = lax.broadcasted_iota(jnp.int32, (n_tok, n_tok), 1)
    earlier = (t_row // tok_dev == t_col // tok_dev) & (t_col < t_row)
    ranks = jnp.dot(
        jnp.where(earlier, 1.0, 0.0).astype(jnp.bfloat16), hits.astype(jnp.bfloat16),
        preferred_element_type=jnp.float32,
    )
    device = (lax.broadcasted_iota(jnp.int32, hits.shape, 0) // tok_dev).astype(jnp.float32)
    seat = lax.rem(lax.broadcasted_iota(jnp.int32, hits.shape, 1), seats).astype(jnp.float32)
    chosen = hit & (CAP * device + ranks == seat)
    one_hot = jnp.where(chosen, 1.0, 0.0).astype(jnp.bfloat16)
    rows = lax.dot_general(one_hot, block, contract_first, preferred_element_type=jnp.float32)
    rows = rows[: row_ids.shape[0]]
    meta_rows = rows[:, 2 * width :]
    gates = sum(pltpu.roll(meta_rows, 128 - top * part, 1) for part in (1, 2, 3))
    lane = lax.broadcasted_iota(jnp.int32, meta_rows.shape, 1)
    gate = jnp.sum(
        jnp.where((lane < top) & (meta_rows == row_ids), gates, 0.0), axis=1, keepdims=True
    )
    return rows[:, :width].astype(jnp.bfloat16), (gate * rows[:, width : 2 * width]).astype(jnp.bfloat16)


def spread_kernel(
    n_cols, own_ref, lane_ref, row_ref, all_ref, held, sent, keep_sem,
    send_p, recv_p, send_m, recv_m, send_s, recv_s,
    keep_x, send_x, recv_x, send_y, recv_y, send_f, recv_f,
):
    e = lax.axis_index("expert")
    chips = n_cols // 2
    order = near_order(chips)
    my_x, my_y, at = xy_peers()
    north, south = at(0, 1), at(0, 3)
    ahead = {"expert": lax.rem(e + 2, n_cols)}
    behind = {"expert": lax.rem(e + n_cols - 2, n_cols)}
    twin = {"expert": e + 1 - 2 * lax.rem(e, 2)}
    tok_dev, full = own_ref.shape
    width = (full - 128) // 2
    groups, slots = sent.shape[0], sent.shape[1]
    seats = sent.shape[2]
    per_group = seats // CAP
    cuts = [pl.ds(0, width), pl.ds(width, width + 128)]
    up_steps, down_steps = chips // 2, chips // 2 - 1
    meet([ahead, behind, twin, at(1, 0), at(2, 0), at(3, 0), north, south])
    started = []

    def go(copy):
        copy.start()
        started.append(copy)

    def spot(shift, other, h):
        index = order.index(shift) * 2 + other
        return held.at[index // per_group, pl.ds(index % per_group * tok_dev, tok_dev), cuts[h]]

    def source(shift, h):
        return own_ref.at[:, cuts[h]] if shift == 0 else spot(shift, 0, h)

    def up(s, h):
        shift = -(s + 1)
        return remote(source(-s, h), spot(shift, 0, h), send_p.at[s, h], recv_p.at[s, h], ahead)

    def down(s, h):
        return remote(source(s, h), spot(s + 1, 0, h), send_m.at[s, h], recv_m.at[s, h], behind)

    def side(shift, h):
        index = order.index(shift)
        return remote(source(shift, h), spot(shift, 1, h), send_s.at[index, h], recv_s.at[index, h], twin)

    x_of = [lax.rem(my_x + k, SLICES) for k in range(SLICES)]
    y_of = [lax.rem(my_y + k, SLICES) for k in range(SLICES)]
    low, high = pl.ds(0, width), pl.ds(width, width)

    def x_copy(g, k):
        back = SLICES - k
        return remote(
            sent.at[g, x_of[k]], all_ref.at[g, my_y, my_x], send_x.at[g, back], recv_x.at[g, back], at(k, 0)
        )

    def y_send(g, k, src):
        block = all_ref.at[g, my_y, x_of[k]]
        go(remote(src, block, send_y.at[g, 0, k], recv_y.at[g, 0, k], north))
        go(remote(src, block, send_y.at[g, 1, k], recv_y.at[g, 1, k], south))

    def x_then_y(g):
        for k in (1, 3, 2):
            block = all_ref.at[g, my_y, x_of[k]]
            remote(block, block, send_x.at[g, k], recv_x.at[g, k], at(k, 0)).wait_recv()
            y_send(g, k, block)

    def pass_on(g):
        for k in (0, 1, 3, 2):
            block = all_ref.at[g, y_of[3], x_of[k]]
            remote(block, block, send_y.at[g, 0, k], recv_y.at[g, 0, k], south).wait_recv()
            part = all_ref.at[g, y_of[3], x_of[k], :, low]
            go(remote(part, part, send_f.at[g, 0, k], recv_f.at[g, 0, k], north))
            block = all_ref.at[g, y_of[1], x_of[k]]
            remote(block, block, send_y.at[g, 1, k], recv_y.at[g, 1, k], north).wait_recv()
            part = all_ref.at[g, y_of[1], x_of[k], :, high]
            go(remote(part, part, send_f.at[g, 1, k], recv_f.at[g, 1, k], south))

    def finish(g):
        for k in (0, 1, 3, 2):
            part = all_ref.at[g, y_of[2], x_of[k], :, low]
            remote(part, part, send_f.at[g, 0, k], recv_f.at[g, 0, k], south).wait_recv()
            part = all_ref.at[g, y_of[2], x_of[k], :, high]
            remote(part, part, send_f.at[g, 1, k], recv_f.at[g, 1, k], north).wait_recv()

    def choose(g):
        for index in range(g * per_group, (g + 1) * per_group):
            if index % 2 == 1:
                for h in range(2):
                    side(order[index // 2], h).wait_recv()
        block = held[g]
        x_rows, d_rows = pick_rows(block, lane_ref[0:1, :], row_ref[...], tok_dev, seats)
        for q in range(slots):
            sent[g, q, :, 0:width] = x_rows[q * seats : (q + 1) * seats]
            sent[g, q, :, width : 2 * width] = d_rows[q * seats : (q + 1) * seats]
        for k in (2, 1, 3):
            go(x_copy(g, k))
        y_send(g, 0, sent.at[g, my_x])
        keep = pltpu.make_async_copy(sent.at[g, my_x], all_ref.at[g, my_y, my_x], keep_x.at[g])
        keep.start()
        keeps.append(keep)

    keeps = []
    for h in range(2):
        go(up(0, h))
        go(down(0, h))
        go(side(0, h))
    own = pltpu.make_async_copy(own_ref, held.at[0, pl.ds(0, tok_dev)], keep_sem)
    own.start()
    own.wait()
    for s in range(1, up_steps + 1):
        for h in range(2):
            up(s - 1, h).wait_recv()
            if s < up_steps:
                go(up(s, h))
            if s <= down_steps:
                down(s - 1, h).wait_recv()
                if s < down_steps:
                    go(down(s, h))
        for h in range(2):
            go(side(-s, h))
            if s <= down_steps:
                go(side(s, h))
        if s % 2 == 0:
            choose(s // 2 - 1)
        elif s > 1:
            g = (s - 3) // 2
            x_then_y(g)
            if g > 0:
                pass_on(g - 1)
    last = groups - 1
    pass_on(last - 1)
    x_then_y(last)
    pass_on(last)
    for g in range(groups):
        finish(g)
    for copy in started:
        copy.wait_send()
    for keep in keeps:
        keep.wait()


def spread_rows(packed, lane_ids, row_ids, n_cols, slots):
    tok_dev, full = packed.shape
    chips = n_cols // 2
    groups = 4
    seats = n_cols * CAP // groups
    width = (full - 128) // 2
    up, down = chips // 2, chips // 2 - 1
    dma = pltpu.SemaphoreType.DMA
    return pl.pallas_call(
        functools.partial(spread_kernel, n_cols),
        out_shape=jax.ShapeDtypeStruct((groups, SLICES, slots, seats, 2 * width), packed.dtype),
        in_specs=[VMEM_SPEC] * 3,
        out_specs=VMEM_SPEC,
        scratch_shapes=[
            pltpu.VMEM((groups, n_cols // groups * tok_dev, full), packed.dtype),
            pltpu.VMEM((groups, slots, seats, 2 * width), packed.dtype),
            dma, dma((up, 2)), dma((up, 2)), dma((down, 2)), dma((down, 2)),
            dma((chips, 2)), dma((chips, 2)),
            dma((groups,)), dma((groups, SLICES)), dma((groups, SLICES)),
            dma((groups, 2, SLICES)), dma((groups, 2, SLICES)),
            dma((groups, 2, SLICES)), dma((groups, 2, SLICES)),
        ],
        compiler_params=pltpu.CompilerParams(collective_id=0, has_side_effects=True),
        cost_estimate=pl.CostEstimate(flops=0, bytes_accessed=200_000_000, transcendentals=0),
        name="spread_rows",
    )(packed, lane_ids, row_ids)


def return_kernel(
    part_ref, back_ref, relay, summed, got, total,
    send_r, recv_r, send_d, recv_d, send_t, recv_t, send_x, recv_x, keep_sem,
):
    my_x, my_y, at = xy_peers()
    north, south = at(0, 1), at(0, 3)
    meet([at(1, 0), at(2, 0), at(3, 0), north, south])
    y_of = [lax.rem(my_y + k, SLICES) for k in range(SLICES)]
    pair = SLICES // 2
    started = []

    def go(copy):
        copy.start()
        started.append(copy)

    def relay_copy(way, i):
        block = pair * (1 - way) + i
        return remote(
            part_ref.at[:, y_of[2], block], relay.at[way, i], send_r.at[way, i], recv_r.at[way, i], (north, south)[way]
        )

    def direct_copy(way, i):
        block = pair * way + i
        return remote(
            part_ref.at[:, y_of[1 if way == 0 else 3], block], got.at[way, block],
            send_d.at[way, i], recv_d.at[way, i], (north, south)[way],
        )

    def total_copy(way, i):
        block = pair * (1 - way) + i
        return remote(
            summed.at[way, i], got.at[way, block], send_t.at[way, i], recv_t.at[way, i], (north, south)[way]
        )

    for i in range(pair):
        for way in range(2):
            go(relay_copy(way, i))
    for i in range(pair):
        for way in range(2):
            go(direct_copy(way, i))
    for i in range(pair):
        for way in range(2):
            relay_copy(way, i).wait_recv()
            block = pair * (1 - way) + i
            mine = part_ref[:, y_of[1 if way == 0 else 3], block].astype(jnp.float32)
            summed[way, i] = (mine + relay[way, i].astype(jnp.float32)).astype(jnp.bfloat16)
            go(total_copy(way, i))
    for i in range(pair):
        for way in range(2):
            direct_copy(way, i).wait_recv()
            total_copy(way, i).wait_recv()
    for k in (2, 1, 3, 0):
        block = lax.rem(my_x + k, SLICES)
        total[block] = (
            part_ref[:, my_y, block].astype(jnp.float32)
            + got[0, block].astype(jnp.float32)
            + got[1, block].astype(jnp.float32)
        ).astype(jnp.bfloat16)
        if k > 0:
            go(remote(
                total.at[block], back_ref.at[my_x], send_x.at[SLICES - k], recv_x.at[SLICES - k], at(k, 0)
            ))
        else:
            keep = pltpu.make_async_copy(total.at[block], back_ref.at[my_x], keep_sem)
            keep.start()
            keep.wait()
    for k in (1, 3, 2):
        block = back_ref.at[lax.rem(my_x + k, SLICES)]
        remote(block, block, send_x.at[k], recv_x.at[k], at(k, 0)).wait_recv()
    for copy in started:
        copy.wait_send()


def return_rows(parts):
    groups, _, slots, seats, width = parts.shape
    dma = pltpu.SemaphoreType.DMA
    pair = SLICES // 2
    return pl.pallas_call(
        return_kernel,
        out_shape=jax.ShapeDtypeStruct((slots, groups, seats, width), parts.dtype),
        in_specs=[VMEM_SPEC],
        out_specs=VMEM_SPEC,
        scratch_shapes=[
            pltpu.VMEM((2, pair, groups, seats, width), jnp.bfloat16),
            pltpu.VMEM((2, pair, groups, seats, width), jnp.bfloat16),
            pltpu.VMEM((2, slots, groups, seats, width), jnp.bfloat16),
            pltpu.VMEM((slots, groups, seats, width), jnp.bfloat16),
        ] + [dma((2, pair))] * 6 + [dma((SLICES,))] * 2 + [dma],
        compiler_params=pltpu.CompilerParams(collective_id=2, has_side_effects=True),
        cost_estimate=pl.CostEstimate(flops=0, bytes_accessed=100_000_000, transcendentals=0),
        name="return_rows",
    )(parts)


def home_kernel(n_cols, rows_ref, home_ref, send_sem, recv_sem, keep_sem):
    e = lax.axis_index("expert")
    chips = n_cols // 2
    order = near_order(chips)
    chip, core = e // 2, lax.rem(e, 2)

    def peer(place):
        z = lax.rem(chip + order[place // 2] + chips, chips)
        return {"expert": 2 * z + (core if place % 2 == 0 else 1 - core)}

    def seen(place):
        shift = -order[place // 2]
        return order.index(shift if shift < chips // 2 else -shift) * 2 + place % 2

    meet([peer(place) for place in range(1, n_cols)])
    for place in reversed(range(1, n_cols)):
        remote(
            rows_ref.at[place], home_ref.at[seen(place)], send_sem.at[seen(place)], recv_sem.at[seen(place)], peer(place)
        ).start()
    keep = pltpu.make_async_copy(rows_ref.at[0], home_ref.at[0], keep_sem)
    keep.start()
    keep.wait()
    for place in range(1, n_cols):
        block = home_ref.at[place]
        remote(block, block, send_sem.at[place], recv_sem.at[place], peer(place)).wait()


def bring_home(rows):
    n_cols = rows.shape[0]
    dma = pltpu.SemaphoreType.DMA
    return pl.pallas_call(
        functools.partial(home_kernel, n_cols),
        out_shape=jax.ShapeDtypeStruct(rows.shape, rows.dtype),
        in_specs=[VMEM_SPEC],
        out_specs=VMEM_SPEC,
        scratch_shapes=[dma((n_cols,)), dma((n_cols,)), dma],
        compiler_params=pltpu.CompilerParams(collective_id=3, has_side_effects=True),
        cost_estimate=pl.CostEstimate(flops=0, bytes_accessed=100_000_000, transcendentals=0),
        name="bring_home",
    )(rows)


def per_device(tokens, upstream, expert_ids, gates, relocate, w_gate_up, w_down):
    n_rows = lax.axis_size("dp")
    n_cols = lax.axis_size("expert")
    slots = n_rows // SLICES
    tok_dev, width = tokens.shape
    top = expert_ids.shape[1]
    slice_width = w_down.shape[2]
    half = n_cols // 2
    seats = n_cols * CAP
    col = lax.axis_index("expert")
    slot_here = lax.axis_index("dp") // SLICES

    meta = jnp.concatenate(
        [expert_ids.astype(jnp.bfloat16)] + three_parts(gates)
        + [jnp.zeros((tok_dev, 128 - 4 * top), jnp.bfloat16)],
        axis=1,
    )
    packed = jnp.concatenate([tokens, upstream, meta], axis=1)
    own_pack = jnp.concatenate([w_gate_up[0, 0], w_down[0, 0]], axis=0)
    far_pack = half_swap(own_pack, n_cols, 0)

    even = col % 2 == 0
    rel_row = jnp.sum(
        jnp.where(jnp.arange(n_cols)[:, None] == col, relocate, 0), axis=0
    )
    served = jnp.where(even, (col + half * rel_row) % n_cols, col) * slots + jnp.arange(slots)
    group_seats = seats // 4
    lanes = jnp.arange(128, dtype=jnp.int32) // group_seats
    lane_ids = jnp.sum(
        jnp.where(lanes[None, :] == jnp.arange(slots)[:, None], served[:, None] + 1, 0), axis=0
    ) - 1
    lane_ids = lane_ids.astype(jnp.float32)
    row_ids = jnp.broadcast_to(lane_ids[: slots * group_seats, None], (slots * group_seats, 128))
    lane_ids = jnp.broadcast_to(lane_ids[None, :], (8, 128))
    spread = spread_rows(packed, lane_ids, row_ids, n_cols, slots)
    all_rows = spread.reshape(-1, 2 * width)
    rows_x = all_rows[:, :width]
    rows_d = all_rows[:, width:]

    rel_here = jnp.sum(jnp.where(jnp.arange(slots) == slot_here, rel_row, 0))
    pack = jnp.where(even & (rel_here == 1), far_pack, own_pack)
    gate_up = pack[: 2 * slice_width]
    down_rows = pack[2 * slice_width :]
    gate_and_up = lax.dot_general(
        rows_x, gate_up, contract_last, preferred_element_type=jnp.float32
    )
    gate_pre = gate_and_up[:, :slice_width]
    up_pre = gate_and_up[:, slice_width:]
    activated, slope_of = silu_parts(gate_pre)
    hidden = (activated * up_pre).astype(jnp.bfloat16)
    hidden_grad = lax.dot_general(
        rows_d, down_rows, contract_last, preferred_element_type=jnp.float32
    )
    pre_grads = jnp.concatenate(
        [
            (hidden_grad * up_pre * slope_of).astype(jnp.bfloat16),
            (hidden_grad * activated).astype(jnp.bfloat16),
        ],
        axis=1,
    )
    slice_part = jnp.dot(pre_grads, gate_up, preferred_element_type=jnp.float32).astype(
        jnp.bfloat16
    )
    grad_gu = lax.dot_general(
        pre_grads, rows_x, contract_first, preferred_element_type=jnp.float32
    ).astype(jnp.bfloat16)
    grad_dn = lax.dot_general(
        hidden, rows_d, contract_first, preferred_element_type=jnp.float32
    ).astype(jnp.bfloat16)
    grad_pack = jnp.concatenate([grad_gu, grad_dn], axis=0)
    slice_part, grad_pack = lax.optimization_barrier((slice_part, grad_pack))
    far_grads = half_swap(grad_pack, n_cols, 1)
    grad_pack = jnp.where(~even & (rel_here == 1), far_grads, grad_pack)

    back = return_rows(slice_part.reshape(*spread.shape[:-1], width))
    rows_home = (
        back.reshape(slots, n_cols, CAP, width).transpose(1, 0, 2, 3).reshape(n_cols, slots * CAP, width)
    )
    home = bring_home(rows_home).reshape(n_cols * slots * CAP, width)

    flat_ids = expert_ids.reshape(-1)
    experts = slots * n_cols
    relocated = jnp.sum(
        jnp.where(flat_ids[:, None] == jnp.arange(experts)[None, :], relocate.reshape(1, experts), 0), axis=1
    )
    home_col = flat_ids // slots
    served_col = jnp.where(home_col % 2 == 0, (home_col + half * relocated) % n_cols, home_col)
    token_of = jnp.arange(flat_ids.shape[0], dtype=jnp.int32) // top
    earlier = (flat_ids[:, None] == flat_ids[None, :]) & (token_of[None, :] < token_of[:, None])
    rank = jnp.sum(earlier.astype(jnp.int32), axis=1)
    chips = n_cols // 2
    shift = (served_col // 2 - col // 2 + chips // 2 + chips) % chips - chips // 2
    place = jnp.minimum(jnp.where(shift > 0, 2 * shift - 1, -2 * shift), chips - 1) * 2
    place = place + (served_col % 2 != col % 2).astype(jnp.int32)
    target = ((place * slots + flat_ids % slots) * CAP + rank).reshape(tok_dev, top)
    picks = jnp.sum(
        (target[:, :, None] == jnp.arange(home.shape[0], dtype=jnp.int32)[None, None, :]).astype(jnp.bfloat16),
        axis=1,
    )
    grad_tokens = jnp.dot(picks, home, preferred_element_type=jnp.float32).astype(jnp.bfloat16)
    return (
        grad_tokens,
        grad_pack[: 2 * slice_width].reshape(w_gate_up.shape),
        grad_pack[2 * slice_width :].reshape(w_down.shape),
    )


def solution(mesh):
    return jax.shard_map(
        per_device,
        mesh=mesh,
        in_specs=(
            P(("dp", "expert"), None),
            P(("dp", "expert"), None),
            P(("dp", "expert"), None),
            P(("dp", "expert"), None),
            P(),
            P("expert", "dp", None, None),
            P("expert", "dp", None, None),
        ),
        out_specs=(
            P(("dp", "expert"), None),
            P("expert", "dp", None, None),
            P("expert", "dp", None, None),
        ),
        check_vma=False,
    )
```

time: 201 us -> 224 us (1.11)
  Pallas kernels: 159 us -> 192 us
  other arithmetic: 10.2 us -> 3.3 us
  local copies, waits for them, and re-layouts: 9.74 us -> 7.31 us
    pallas_call x3 -> x2, Pallas kernels: 117 us -> 143 us  [the longest x1 118 us: spread_rows(): pl.pallas_call(functools.partial(spread_kernel, n_cols), out_shape=jax.Sh...]
    pallas_call x1, Pallas kernels: 42.6 us -> 49.5 us  [bring_home(): pl.pallas_call(functools.partial(home_kernel, n_cols), out_shape=jax.Shap...]
  transfers between devices with their start and end apart: 2 -> 2, of which waited for: 0 -> 0; matrix products, arithmetic and copies ran while one was open for 8% -> 4% of each run, Pallas kernels for 58% -> 86%
where the time goes in v3:
time: 224 us
  Pallas kernels  192 us (86%)
  matrix products  9.94 us (4%)
  starting transfers between devices  9.48 us (4%)
  local copies, waits for them, and re-layouts  7.31 us (3%)
  other arithmetic  3.3 us (1%)
    pallas_call x1, Pallas kernels, spread_rows(): pl.pallas_call(functools.partial(spread_kernel, n_cols), out_shape=jax.Sh...  118 us
    pallas_call x1, Pallas kernels, bring_home(): pl.pallas_call(functools.partial(home_kernel, n_cols), out_shape=jax.Shap...  49.5 us
    pallas_call x1, Pallas kernels, return_rows(): pl.pallas_call(return_kernel, out_shape=jax.ShapeDtypeStruct((slots, grou...  24.1 us
    ppermute x2, starting transfers between devices, half_swap(): return lax.ppermute(block, 'expert', route)  9.48 us
  transfers between devices with their start and end apart: 2, of which 0 were waited for; matrix products, arithmetic and copies ran while one was open for 4% of the time, Pallas kernels for 86%

profile of v3, /device:TPU:1, one launch (start us, length us, event | category | flops | bytes accessed | tf_op | source)
XLA Modules:
  0.0 223.6 jit_solution(14040936231502265277)
XLA Ops:
  0.6 0.0 copy-start.5
  0.6 0.0 copy-start.7
  0.7 0.0 copy-start.6
  0.7 0.0 copy-start.4
  0.7 0.0 copy-start.3
  0.7 1.4 pad_maximum_fusion
  2.0 0.7 collective-permute-start
  2.8 0.0 copy-done.5
  2.8 0.1 copy.47
  2.9 0.0 copy-done.7
  2.9 0.1 select_reduce_fusion.2
  3.0 0.6 add_add_fusion
  4.3 0.0 copy-done.6
  4.3 0.1 copy.49
  4.4 0.1 copy.46
  4.5 0.0 copy-done.4
  4.5 0.0 copy-done.3
  4.5 0.7 concatenate.12.own_ref
  5.3 0.1 select_reduce_fusion.1
  5.3 0.6 broadcast_in_dim.73.lane_ref
  5.9 0.7 broadcast_in_dim.74.row_ref
  6.6 0.0 copy-start.1
  6.6 0.0 copy-start.2
  6.6 118.5 %spread_rows.1 = bf16[4,4,4,16,2048]{4,3,2,1,0:T(8,128)(2,1)} custom-call(bf16[16,2176]{1,0:T(8,128)(2,1)} %concatenate.12.own_ref, f32[8,128]{1,0:T(8,128)} %broadcast_in_dim.73.lane_ref, f32[64,128]{1,0:T(8,128)} %broadcast_in_dim.74.row_ref), custom_call_target="tpu_custom_call" | custom-call | bytes 200000000 | tf_op jit(solution)/shard_map/spread_rows/pallas_call | solution.py:248
  125.1 0.0 collective-permute-done
  125.1 0.0 copy-done.1
  125.2 0.0 copy-done.2
  125.2 0.5 broadcast_select_fusion.1
  125.7 0.0 copy-start
  125.7 2.8 %fusion.2 = f32[1024,384]{0,1:T(8,128)S(1)} fusion(bf16[1024,2048]{1,0:T(8,128)(2,1)} %bitcast.18, bf16[576,1024]{1,0:T(8,128)(2,1)S(1)} %broadcast_select_fusion.1), kind=kOutput, calls=%fused_computation.3 | convolution fusion | flops 805306368 | bytes 4456448 | tf_op jit(solution)/shard_map/dot_general | solution.py:447
  128.4 0.0 copy-done
  128.5 0.6 fusion.11
  129.1 1.1 multiply_convert_fusion.2
  130.2 1.0 fusion.8
  131.2 2.6 %convolution_convert_fusion = bf16[1024,1024]{1,0:T(8,128)(2,1)} fusion(bf16[576,1024]{1,0:T(8,128)(2,1)S(1)} %broadcast_select_fusion.1, bf16[1024,192]{0,1:T(8,128)(2,1)S(1)} %get-tuple-element.10, bf16[1024,192]{0,1:T(8,128)(2,1)S(1)} %get-tuple-element.9), kind=kOutput, calls=%fused_computation | convolution fusion | flops 807927808 | bytes 3670016 | tf_op jit(solution)/shard_map/dot_general | solution.py:464
  133.8 0.1 pad_maximum_fusion.1
  133.9 8.7 %collective-permute-start.1 = (bf16[576,1024]{1,0:T(8,128)(2,1)S(1)}, bf16[576,1024]{1,0:T(8,128)(2,1)S(1)}, u32[]{:S(2)}, u32[]{:S(2)}) collective-permute-start(bf16[576,1024]{1,0:T(8,128)(2,1)S(1)} %pad_maximum_fusion.1), channel_id=1, source_target_pairs={{1,17},{3,19},{5,21},{7,23},{9,25},{11,27},{13,29},{15,31},{17,1},... | collective-permute-start | bytes 3538952 | tf_op jit(solution)/shard_map/ppermute | solution.py:27
  142.7 0.1 copy.40
  142.8 0.1 copy.45
  142.8 0.1 eq.93
  142.9 0.1 broadcast_in_dim.65
  143.1 0.2 select_reduce_fusion
  143.2 0.1 mul.73
  143.3 0.1 reduce_sum.61
  143.4 0.1 fusion.34
  143.5 0.1 fusion.21
  143.6 24.1 %return_rows.1 = bf16[4,4,16,1024]{3,2,1,0:T(8,128)(2,1)} custom-call(bf16[4,4,4,16,1024]{4,3,2,1,0:T(8,128)(2,1)} %bitcast.24), custom_call_target="tpu_custom_call" | custom-call | bytes 100000000 | tf_op jit(solution)/shard_map/return_rows/pallas_call | solution.py:345
  167.7 1.2 reshape.219
  168.9 0.5 copy.52
  169.5 1.0 reshape.220.rows_ref
  170.5 49.5 %bring_home.1 = bf16[32,8,1024]{2,1,0:T(8,128)(2,1)} custom-call(bf16[32,8,1024]{2,1,0:T(8,128)(2,1)} %reshape.220.rows_ref), custom_call_target="tpu_custom_call" | custom-call | bytes 100000000 | tf_op jit(solution)/shard_map/bring_home/pallas_call | solution.py:392
  220.0 1.8 convolution_convert_fusion.1
  221.8 0.0 collective-permute-done.1
  221.8 0.1 broadcast_select_fusion
  221.9 0.8 slice_bitcast_fusion.1
  222.7 0.9 slice_bitcast_fusion
  (9 shorter events, 0.0 us)
Async XLA Ops:
  0.6 2.2 copy-start.5
  0.6 2.3 %copy-start.7 = (s32[32,4]{0,1:T(4,128)S(1)}, s32[32,4]{0,1:T(4,128)}, u32[]{:S(2)}) copy-start(s32[32,4]{0,1:T(4,128)} %param.11) | copy-start | bytes 1540
  0.7 3.7 %copy-start.6 = (s32[16,8]{0,1:T(8,128)S(1)}, s32[16,8]{0,1:T(8,128)}, u32[]{:S(2)}) copy-start(s32[16,8]{0,1:T(8,128)} %param.9) | copy-start | bytes 1540
  0.7 3.8 %copy-start.4 = (bf16[16,1024]{1,0:T(8,128)(2,1)S(1)}, bf16[16,1024]{1,0:T(8,128)(2,1)}, u32[]{:S(2)}) copy-start(bf16[16,1024]{1,0:T(8,128)(2,1)} %param.8) | copy-start | bytes 98308
  0.7 3.8 %copy-start.3 = (bf16[16,1024]{1,0:T(8,128)(2,1)S(1)}, bf16[16,1024]{1,0:T(8,128)(2,1)}, u32[]{:S(2)}) copy-start(bf16[16,1024]{1,0:T(8,128)(2,1)} %param.7) | copy-start | bytes 98308
  2.0 123.1 %collective-permute-start = (bf16[576,1024]{1,0:T(8,128)(2,1)S(1)}, bf16[576,1024]{1,0:T(8,128)(2,1)S(1)}, u32[]{:S(2)}, u32[]{:S(2)}) collective-permute-start(bf16[576,1024]{1,0:T(8,128)(2,1)S(1)} %pad_maximum_fusion), channel_id=1, source_target_pairs={{0,16},{2,18},{4,20},{6,22},{8,24},{10,26},{12,28},{14,30},{16,0},... | collective-permute-start | bytes 3538952 | tf_op jit(solution)/shard_map/ppermute | solution.py:27
  6.6 118.5 %copy-start.1 = (bf16[1,1,384,1024]{3,2,1,0:T(8,128)(2,1)S(1)}, bf16[1,1,384,1024]{3,2,1,0:T(8,128)(2,1)}, u32[]{:S(2)}) copy-start(bf16[1,1,384,1024]{3,2,1,0:T(8,128)(2,1)} %param.12) | copy-start | bytes 2359300
  6.6 118.5 %copy-start.2 = (bf16[1,1,192,1024]{3,2,1,0:T(8,128)(2,1)S(1)}, bf16[1,1,192,1024]{3,2,1,0:T(8,128)(2,1)}, u32[]{:S(2)}) copy-start(bf16[1,1,192,1024]{3,2,1,0:T(8,128)(2,1)} %param.13) | copy-start | bytes 1179652
  125.7 2.8 %copy-start = (bf16[4,4,4,16,2048]{4,3,2,1,0:T(8,128)(2,1)S(1)}, bf16[4,4,4,16,2048]{4,3,2,1,0:T(8,128)(2,1)}, u32[]{:S(2)}) copy-start(bf16[4,4,4,16,2048]{4,3,2,1,0:T(8,128)(2,1)} %spread_rows.1) | copy-start | bytes 12582916
  133.9 87.9 %collective-permute-start.1 = (bf16[576,1024]{1,0:T(8,128)(2,1)S(1)}, bf16[576,1024]{1,0:T(8,128)(2,1)S(1)}, u32[]{:S(2)}, u32[]{:S(2)}) collective-permute-start(bf16[576,1024]{1,0:T(8,128)(2,1)S(1)} %pad_maximum_fusion.1), channel_id=1, source_target_pairs={{1,17},{3,19},{5,21},{7,23},{9,25},{11,27},{13,29},{15,31},{17,1},... | collective-permute-start | bytes 3538952 | tf_op jit(solution)/shard_map/ppermute | solution.py:27

commit v4 on v3

v4 whole, which is shorter than its diff:
```python
import functools

import jax
import jax.numpy as jnp
from jax import lax
from jax.experimental import pallas as pl
from jax.experimental.pallas import tpu as pltpu
from jax.sharding import PartitionSpec as P

SLICES = 4
CAP = 2
MESH = pl.DeviceIdType.MESH

contract_last = (((1,), (1,)), ((), ()))
contract_first = (((0,), (0,)), ((), ()))
VMEM_SPEC = pl.BlockSpec(memory_space=pltpu.VMEM)


def silu_parts(values_in):
    sigmoid_of = jax.nn.sigmoid(values_in)
    return (values_in * sigmoid_of, sigmoid_of * (1.0 + values_in * (1.0 - sigmoid_of)))


def half_swap(block, count, parity):
    half = count // 2
    route = [(c, (c + half) % count) for c in range(count) if c % 2 == parity]
    return lax.ppermute(block, "expert", route)


def three_parts(gates):
    first = lax.reduce_precision(gates, 8, 7)
    rest = gates - first
    second = lax.reduce_precision(rest, 8, 7)
    third = rest - second
    return [part.astype(jnp.bfloat16) for part in (first, second, third)]


def meet(peers):
    barrier = pltpu.get_barrier_semaphore()
    for peer in peers:
        pl.semaphore_signal(barrier, inc=1, device_id=peer, device_id_type=MESH)
    pl.semaphore_wait(barrier, len(peers))


def remote(src, dst, send_sem, recv_sem, peer):
    return pltpu.make_async_remote_copy(
        src_ref=src, dst_ref=dst, send_sem=send_sem, recv_sem=recv_sem,
        device_id=peer, device_id_type=MESH,
    )


def xy_peers():
    row = lax.axis_index("dp")
    my_x, my_y = row // SLICES, lax.rem(row, SLICES)

    def at(dx, dy):
        return {"dp": lax.rem(my_x + dx, SLICES) * SLICES + lax.rem(my_y + dy, SLICES)}

    return my_x, my_y, at


def near_order(chips):
    order = [0]
    for s in range(1, chips // 2):
        order += [s, -s]
    return order + [-(chips // 2)]


def pick_rows(block, lane_ids, row_ids, tok_dev, seats):
    n_tok, width = block.shape[0], (block.shape[1] - 128) // 2
    top = 8
    meta = block[:, 2 * width :].astype(jnp.float32)
    hit = meta[:, 0:1] == lane_ids
    for k in range(1, top):
        hit = hit | (meta[:, k : k + 1] == lane_ids)
    hits = jnp.where(hit, 1.0, 0.0)
    t_row = lax.broadcasted_iota(jnp.int32, (n_tok, n_tok), 0)
    t_col = lax.broadcasted_iota(jnp.int32, (n_tok, n_tok), 1)
    earlier = (t_row // tok_dev == t_col // tok_dev) & (t_col < t_row)
    ranks = jnp.dot(
        jnp.where(earlier, 1.0, 0.0).astype(jnp.bfloat16), hits.astype(jnp.bfloat16),
        preferred_element_type=jnp.float32,
    )
    device = (lax.broadcasted_iota(jnp.int32, hits.shape, 0) // tok_dev).astype(jnp.float32)
    seat = lax.rem(lax.broadcasted_iota(jnp.int32, hits.shape, 1), seats).astype(jnp.float32)
    chosen = hit & (CAP * device + ranks == seat)
    one_hot = jnp.where(chosen, 1.0, 0.0).astype(jnp.bfloat16)
    rows = lax.dot_general(one_hot, block, contract_first, preferred_element_type=jnp.float32)
    rows = rows[: row_ids.shape[0]]
    meta_rows = rows[:, 2 * width :]
    gates = sum(pltpu.roll(meta_rows, 128 - top * part, 1) for part in (1, 2, 3))
    lane = lax.broadcasted_iota(jnp.int32, meta_rows.shape, 1)
    gate = jnp.sum(
        jnp.where((lane < top) & (meta_rows == row_ids), gates, 0.0), axis=1, keepdims=True
    )
    return rows[:, :width].astype(jnp.bfloat16), (gate * rows[:, width : 2 * width]).astype(jnp.bfloat16)


def moves_weights(e):
    return lax.rem(e, 2) == 0


def step_kernel(
    n_cols, own_ref, lane_ref, row_ref, flag_ref, picks_ref, gate_up_ref, down_ref,
    tokens_ref, grads_ref, far_grads,
    held, sent, rows_in, weights, far_weights, da_all, db_all, hidden_all,
    part_ref, relay, summed, got, total, back, places, home,
    keep_sem, send_p, recv_p, send_m, recv_m, send_s, recv_s,
    keep_x, send_x, recv_x, send_y, recv_y, send_f, recv_f,
    load_w, send_w, recv_w, send_g, recv_g,
    send_r, recv_r, send_d, recv_d, send_t, recv_t, send_b, recv_b, keep_b,
    send_h, recv_h, keep_h,
):
    e = lax.axis_index("expert")
    chips = n_cols // 2
    order = near_order(chips)
    chip, core = e // 2, lax.rem(e, 2)
    my_x, my_y, at = xy_peers()
    north, south = at(0, 1), at(0, 3)
    ahead = {"expert": lax.rem(e + 2, n_cols)}
    behind = {"expert": lax.rem(e + n_cols - 2, n_cols)}
    twin = {"expert": e + 1 - 2 * core}
    across = {"expert": lax.rem(e + chips, n_cols)}
    tok_dev, full = own_ref.shape
    width = (full - 128) // 2
    groups, slots = sent.shape[0], sent.shape[1]
    seats = sent.shape[2]
    block_rows = SLICES * slots * seats
    per_group = seats // CAP
    f_slice = down_ref.shape[0]
    quarter = width // 2
    cuts = [
        pl.ds(0, quarter), pl.ds(quarter, quarter), pl.ds(2 * quarter, quarter), pl.ds(3 * quarter, quarter + 128)
    ]
    n_cut = len(cuts)
    up_steps, down_steps = chips // 2, chips // 2 - 1
    early = moves_weights(e)

    def peer(place):
        z = lax.rem(chip + order[place // 2] + chips, chips)
        return {"expert": 2 * z + (core if place % 2 == 0 else 1 - core)}

    def seen(place):
        shift = -order[place // 2]
        return order.index(shift if shift < chips // 2 else -shift) * 2 + place % 2

    meet([peer(place) for place in range(1, n_cols)] + [at(1, 0), at(2, 0), at(3, 0), north, south])
    started = []

    def go(copy):
        copy.start()
        started.append(copy)

    def landed(ref, send_sem, recv_sem, who):
        remote(ref, ref, send_sem, recv_sem, who).wait_recv()

    def spot(shift, other, h):
        index = order.index(shift) * 2 + other
        return held.at[index // per_group, pl.ds(index % per_group * tok_dev, tok_dev), cuts[h]]

    def source(shift, h):
        return own_ref.at[:, cuts[h]] if shift == 0 else spot(shift, 0, h)

    def up(s, h):
        return remote(source(-s, h), spot(-(s + 1), 0, h), send_p.at[s, h], recv_p.at[s, h], ahead)

    def down(s, h):
        return remote(source(s, h), spot(s + 1, 0, h), send_m.at[s, h], recv_m.at[s, h], behind)

    def side(shift, h):
        index = order.index(shift)
        return remote(source(shift, h), spot(shift, 1, h), send_s.at[index, h], recv_s.at[index, h], twin)

    x_of = [lax.rem(my_x + k, SLICES) for k in range(SLICES)]
    y_of = [lax.rem(my_y + k, SLICES) for k in range(SLICES)]
    low, high = pl.ds(0, width), pl.ds(width, width)

    def x_copy(g, k):
        far = SLICES - k
        return remote(
            sent.at[g, x_of[k]], rows_in.at[g, my_y, my_x], send_x.at[g, far], recv_x.at[g, far], at(k, 0)
        )

    def y_send(g, k, src):
        block = rows_in.at[g, my_y, x_of[k]]
        go(remote(src, block, send_y.at[g, 0, k], recv_y.at[g, 0, k], north))
        go(remote(src, block, send_y.at[g, 1, k], recv_y.at[g, 1, k], south))

    def x_then_y(g):
        for k in (1, 3, 2):
            block = rows_in.at[g, my_y, x_of[k]]
            landed(block, send_x.at[g, k], recv_x.at[g, k], at(k, 0))
            y_send(g, k, block)

    def pass_on(g):
        for k in (0, 1, 3, 2):
            landed(rows_in.at[g, y_of[3], x_of[k]], send_y.at[g, 0, k], recv_y.at[g, 0, k], south)
            part = rows_in.at[g, y_of[3], x_of[k], :, low]
            go(remote(part, part, send_f.at[g, 0, k], recv_f.at[g, 0, k], north))
            landed(rows_in.at[g, y_of[1], x_of[k]], send_y.at[g, 1, k], recv_y.at[g, 1, k], north)
            part = rows_in.at[g, y_of[1], x_of[k], :, high]
            go(remote(part, part, send_f.at[g, 1, k], recv_f.at[g, 1, k], south))

    def finish(g):
        for k in (0, 1, 3, 2):
            landed(rows_in.at[g, y_of[2], x_of[k], :, low], send_f.at[g, 0, k], recv_f.at[g, 0, k], south)
            landed(rows_in.at[g, y_of[2], x_of[k], :, high], send_f.at[g, 1, k], recv_f.at[g, 1, k], north)

    keeps = []

    def choose(g):
        for index in range(g * per_group, (g + 1) * per_group):
            if index % 2 == 1:
                for h in range(n_cut):
                    side(order[index // 2], h).wait_recv()
        x_rows, d_rows = pick_rows(held[g], lane_ref[0:1, :], row_ref[...], tok_dev, seats)
        for q in range(slots):
            sent[g, q, :, 0:width] = x_rows[q * seats : (q + 1) * seats]
            sent[g, q, :, width : 2 * width] = d_rows[q * seats : (q + 1) * seats]
        for k in (2, 1, 3):
            go(x_copy(g, k))
        y_send(g, 0, sent.at[g, my_x])
        keep = pltpu.make_async_copy(sent.at[g, my_x], rows_in.at[g, my_y, my_x], keep_x.at[g])
        keep.start()
        keeps.append(keep)

    for h in range(n_cut):
        go(up(0, h))
        go(down(0, h))
        go(side(0, h))
    own = pltpu.make_async_copy(own_ref, held.at[0, pl.ds(0, tok_dev)], keep_sem)
    own.start()
    gate_up_at, down_at = pl.ds(0, 2 * f_slice), pl.ds(2 * f_slice, f_slice)
    loads = [
        pltpu.make_async_copy(gate_up_ref, weights.at[gate_up_at], load_w.at[0]),
        pltpu.make_async_copy(down_ref, weights.at[down_at], load_w.at[1]),
    ]
    for load in loads:
        load.start()
    own.wait()
    for s in range(1, up_steps + 1):
        for h in range(n_cut):
            up(s - 1, h).wait_recv()
            if s < up_steps:
                go(up(s, h))
            if s <= down_steps:
                down(s - 1, h).wait_recv()
                if s < down_steps:
                    go(down(s, h))
        for h in range(n_cut):
            go(side(-s, h))
            if s <= down_steps:
                go(side(s, h))
        if s == up_steps:
            w_copies = [
                remote(gate_up_ref, far_weights.at[gate_up_at], send_w.at[0], recv_w.at[0], across),
                remote(down_ref, far_weights.at[down_at], send_w.at[1], recv_w.at[1], across),
            ]

            @pl.when(early)
            def _():
                for copy in w_copies:
                    copy.start()

        if s % 2 == 0:
            choose(s // 2 - 1)
        elif s > 1:
            g = (s - 3) // 2
            x_then_y(g)
            if g > 0:
                pass_on(g - 1)
    last = groups - 1
    pass_on(last - 1)
    x_then_y(last)
    pass_on(last)
    for g in range(groups):
        finish(g)
    for keep in keeps:
        keep.wait()
    for load in loads:
        load.wait()

    @pl.when(early)
    def _():
        for copy in w_copies:
            copy.wait()
        moved = jnp.broadcast_to(flag_ref[0:1, 0:1], (f_slice, width)) > 0.5
        for i in range(3):
            at_rows = pl.ds(i * f_slice, f_slice)
            weights[at_rows] = jnp.where(
                moved, far_weights[at_rows].astype(jnp.float32), weights[at_rows].astype(jnp.float32)
            ).astype(jnp.bfloat16)

    w_gate, w_up, w_down = (pl.ds(i * f_slice, f_slice) for i in range(3))

    def x_and_d(g):
        block = rows_in[g].reshape(block_rows, 2 * width)
        return block[:, :width], block[:, width:]

    def forward(g, _):
        x, d = x_and_d(g)
        dot = functools.partial(lax.dot_general, dimension_numbers=contract_last, preferred_element_type=jnp.float32)
        up_pre = dot(x, weights[w_up])
        activated, slope_of = silu_parts(dot(x, weights[w_gate]))
        hidden_grad = dot(d, weights[w_down])
        hidden_all[g] = (activated * up_pre).astype(jnp.bfloat16)
        da_all[g] = (hidden_grad * up_pre * slope_of).astype(jnp.bfloat16)
        db_all[g] = (hidden_grad * activated).astype(jnp.bfloat16)
        return 0

    lax.fori_loop(0, groups, forward, 0)
    every_row = rows_in[...].reshape(groups * block_rows, 2 * width)
    g_copies = []
    for i, (left, lo) in enumerate(((da_all, 0), (db_all, 0), (hidden_all, width))):
        at_rows = pl.ds(i * f_slice, f_slice)
        grads_ref[at_rows] = lax.dot_general(
            left[...].reshape(groups * block_rows, f_slice), every_row[:, lo : lo + width], contract_first,
            preferred_element_type=jnp.float32,
        ).astype(jnp.bfloat16)
        g_copies.append(
            remote(grads_ref.at[at_rows], far_grads.at[at_rows], send_g.at[i], recv_g.at[i], across)
        )

    @pl.when(jnp.logical_not(early))
    def _():
        for copy in g_copies:
            copy.start()

    pair = SLICES // 2

    def relay_copy(g, way, i):
        block = pair * (1 - way) + i
        return remote(
            part_ref.at[g, y_of[2], block], relay.at[g, way, i], send_r.at[g, way, i], recv_r.at[g, way, i],
            (north, south)[way],
        )

    def direct_copy(g, way, i):
        block = pair * way + i
        return remote(
            part_ref.at[g, y_of[1 if way == 0 else 3], block], got.at[g, way, block],
            send_d.at[g, way, i], recv_d.at[g, way, i], (north, south)[way],
        )

    def total_copy(g, way, i):
        block = pair * (1 - way) + i
        return remote(
            summed.at[g, way, i], got.at[g, way, block], send_t.at[g, way, i], recv_t.at[g, way, i],
            (north, south)[way],
        )

    every = [(way, i) for i in range(pair) for way in range(2)]
    for g in range(groups):
        part = jnp.dot(
            da_all[g], weights[w_gate], preferred_element_type=jnp.float32
        ) + jnp.dot(db_all[g], weights[w_up], preferred_element_type=jnp.float32)
        part_ref[g] = part.astype(jnp.bfloat16).reshape(SLICES, slots, seats, width)
        for way, i in every:
            go(relay_copy(g, way, i))
        for way, i in every:
            go(direct_copy(g, way, i))
    for g in range(groups):
        for way, i in every:
            relay_copy(g, way, i).wait_recv()
            mine = part_ref[g, y_of[1 if way == 0 else 3], pair * (1 - way) + i].astype(jnp.float32)
            summed[g, way, i] = (mine + relay[g, way, i].astype(jnp.float32)).astype(jnp.bfloat16)
            go(total_copy(g, way, i))
    back_keeps = []

    per_place = slots * CAP
    n_rows = slots * seats
    to_row = lax.broadcasted_iota(jnp.int32, (n_rows, n_rows), 0)
    from_row = lax.broadcasted_iota(jnp.int32, (n_rows, n_rows), 1)
    wanted = (to_row % per_place) // CAP * seats + to_row // per_place * CAP + to_row % CAP
    regroup = jnp.where(from_row == wanted, 1.0, 0.0).astype(jnp.bfloat16)

    def send_home(g):
        for k in (1, 3, 2):
            landed(back.at[g, x_of[k]], send_b.at[g, k], recv_b.at[g, k], at(k, 0))
        back_keeps[g].wait()
        rows = jnp.dot(
            regroup, back[g].reshape(n_rows, width), preferred_element_type=jnp.float32
        ).astype(jnp.bfloat16)
        places[pl.ds(g * per_group, per_group)] = rows.reshape(per_group, per_place, width)
        for place in reversed(range(g * per_group, (g + 1) * per_group)):
            if place > 0:
                go(remote(
                    places.at[place], home.at[seen(place)], send_h.at[seen(place)], recv_h.at[seen(place)], peer(place)
                ))

    for g in range(groups):
        for way, i in every:
            direct_copy(g, way, i).wait_recv()
            total_copy(g, way, i).wait_recv()
        for k in (2, 1, 3, 0):
            block = x_of[k]
            total[g, block] = (
                part_ref[g, my_y, block].astype(jnp.float32)
                + got[g, 0, block].astype(jnp.float32)
                + got[g, 1, block].astype(jnp.float32)
            ).astype(jnp.bfloat16)
            if k > 0:
                far = SLICES - k
                go(remote(
                    total.at[g, block], back.at[g, my_x], send_b.at[g, far], recv_b.at[g, far], at(k, 0)
                ))
            else:
                keep = pltpu.make_async_copy(total.at[g, block], back.at[g, my_x], keep_b.at[g])
                keep.start()
                back_keeps.append(keep)
        if g > 0:
            send_home(g - 1)
    send_home(groups - 1)
    keep = pltpu.make_async_copy(places.at[0], home.at[0], keep_h)
    keep.start()
    keep.wait()
    for place in range(1, n_cols):
        landed(home.at[place], send_h.at[place], recv_h.at[place], peer(place))
    tokens_ref[...] = jnp.dot(
        picks_ref[...], home[...].reshape(n_cols * per_place, width), preferred_element_type=jnp.float32
    ).astype(tokens_ref.dtype)

    @pl.when(jnp.logical_not(early))
    def _():
        for copy in g_copies:
            copy.wait()

    for copy in started:
        copy.wait_send()


def whole_step(packed, lane_ids, row_ids, flag, picks, gate_up, down, n_cols, slots):
    tok_dev, full = packed.shape
    chips = n_cols // 2
    groups = 4
    seats = n_cols * CAP // groups
    width = (full - 128) // 2
    f_slice = down.shape[0]
    block_rows = SLICES * slots * seats
    pair = SLICES // 2
    up, down_steps = chips // 2, chips // 2 - 1
    cut = 4
    bf16 = jnp.bfloat16
    dma = pltpu.SemaphoreType.DMA
    any_spec = pl.BlockSpec(memory_space=pl.ANY)
    grads = jax.ShapeDtypeStruct((3 * f_slice, width), bf16)
    return pl.pallas_call(
        functools.partial(step_kernel, n_cols),
        out_shape=(jax.ShapeDtypeStruct((tok_dev, width), bf16), grads, grads),
        in_specs=[VMEM_SPEC] * 5 + [any_spec] * 2,
        out_specs=(VMEM_SPEC,) * 3,
        scratch_shapes=[
            pltpu.VMEM((groups, n_cols // groups * tok_dev, full), bf16),
            pltpu.VMEM((groups, slots, seats, 2 * width), bf16),
            pltpu.VMEM((groups, SLICES, slots, seats, 2 * width), bf16),
            pltpu.VMEM((3 * f_slice, width), bf16),
            pltpu.VMEM((3 * f_slice, width), bf16),
            pltpu.VMEM((groups, block_rows, f_slice), bf16),
            pltpu.VMEM((groups, block_rows, f_slice), bf16),
            pltpu.VMEM((groups, block_rows, f_slice), bf16),
            pltpu.VMEM((groups, SLICES, slots, seats, width), bf16),
            pltpu.VMEM((groups, 2, pair, seats, width), bf16),
            pltpu.VMEM((groups, 2, pair, seats, width), bf16),
            pltpu.VMEM((groups, 2, slots, seats, width), bf16),
            pltpu.VMEM((groups, slots, seats, width), bf16),
            pltpu.VMEM((groups, slots, seats, width), bf16),
            pltpu.VMEM((n_cols, slots * CAP, width), bf16),
            pltpu.VMEM((n_cols, slots * CAP, width), bf16),
            dma, dma((up, cut)), dma((up, cut)), dma((down_steps, cut)), dma((down_steps, cut)),
            dma((chips, cut)), dma((chips, cut)),
            dma((groups,)), dma((groups, SLICES)), dma((groups, SLICES)),
            dma((groups, 2, SLICES)), dma((groups, 2, SLICES)),
            dma((groups, 2, SLICES)), dma((groups, 2, SLICES)),
            dma((2,)), dma((2,)), dma((2,)), dma((3,)), dma((3,)),
        ] + [dma((groups, 2, pair))] * 6 + [
            dma((groups, SLICES)), dma((groups, SLICES)), dma((groups,)),
            dma((n_cols,)), dma((n_cols,)), dma,
        ],
        compiler_params=pltpu.CompilerParams(
            collective_id=0, has_side_effects=True, vmem_limit_bytes=56 * 1024 * 1024
        ),
        name="whole_step",
    )(packed, lane_ids, row_ids, flag, picks, gate_up, down)


def per_device(tokens, upstream, expert_ids, gates, relocate, w_gate_up, w_down):
    n_rows = lax.axis_size("dp")
    n_cols = lax.axis_size("expert")
    slots = n_rows // SLICES
    tok_dev, width = tokens.shape
    top = expert_ids.shape[1]
    slice_width = w_down.shape[2]
    half = n_cols // 2
    seats = n_cols * CAP
    col = lax.axis_index("expert")
    slot_here = lax.axis_index("dp") // SLICES

    meta = jnp.concatenate(
        [expert_ids.astype(jnp.bfloat16)] + three_parts(gates)
        + [jnp.zeros((tok_dev, 128 - 4 * top), jnp.bfloat16)],
        axis=1,
    )
    packed = jnp.concatenate([tokens, upstream, meta], axis=1)
    early = moves_weights(col)
    rel_row = jnp.sum(
        jnp.where(jnp.arange(n_cols)[:, None] == col, relocate, 0), axis=0
    )
    served = jnp.where(early, (col + half * rel_row) % n_cols, col) * slots + jnp.arange(slots)
    group_seats = seats // 4
    lanes = jnp.arange(128, dtype=jnp.int32) // group_seats
    lane_ids = jnp.sum(
        jnp.where(lanes[None, :] == jnp.arange(slots)[:, None], served[:, None] + 1, 0), axis=0
    ) - 1
    lane_ids = lane_ids.astype(jnp.float32)
    row_ids = jnp.broadcast_to(lane_ids[: slots * group_seats, None], (slots * group_seats, 128))
    lane_ids = jnp.broadcast_to(lane_ids[None, :], (8, 128))
    rel_here = jnp.sum(jnp.where(jnp.arange(slots) == slot_here, rel_row, 0))

    flat_ids = expert_ids.reshape(-1)
    experts = slots * n_cols
    relocated = jnp.sum(
        jnp.where(flat_ids[:, None] == jnp.arange(experts)[None, :], relocate.reshape(1, experts), 0), axis=1
    )
    home_col = flat_ids // slots
    served_col = jnp.where(moves_weights(home_col), (home_col + half * relocated) % n_cols, home_col)
    token_of = jnp.arange(flat_ids.shape[0], dtype=jnp.int32) // top
    earlier = (flat_ids[:, None] == flat_ids[None, :]) & (token_of[None, :] < token_of[:, None])
    rank = jnp.sum(earlier.astype(jnp.int32), axis=1)
    chips = n_cols // 2
    shift = (served_col // 2 - col // 2 + chips // 2 + chips) % chips - chips // 2
    place = jnp.minimum(jnp.where(shift > 0, 2 * shift - 1, -2 * shift), chips - 1) * 2
    place = place + (served_col % 2 != col % 2).astype(jnp.int32)
    target = ((place * slots + flat_ids % slots) * CAP + rank).reshape(tok_dev, top)
    n_home = n_cols * slots * CAP
    picks = jnp.sum(
        (target[:, :, None] == jnp.arange(n_home, dtype=jnp.int32)[None, None, :]).astype(jnp.bfloat16),
        axis=1,
    )
    flag = jnp.broadcast_to(rel_here.astype(jnp.float32), (8, 128))
    grad_tokens, near, far = whole_step(
        packed, lane_ids, row_ids, flag, picks, w_gate_up[0, 0], w_down[0, 0], n_cols, slots
    )
    came = ~early & (rel_here == 1)
    gate_up_rows = 2 * slice_width
    return (
        grad_tokens,
        jnp.where(came, far[:gate_up_rows], near[:gate_up_rows]).reshape(w_gate_up.shape),
        jnp.where(came, far[gate_up_rows:], near[gate_up_rows:]).reshape(w_down.shape),
    )


def solution(mesh):
    return jax.shard_map(
        per_device,
        mesh=mesh,
        in_specs=(
            P(("dp", "expert"), None),
            P(("dp", "expert"), None),
            P(("dp", "expert"), None),
            P(("dp", "expert"), None),
            P(),
            P("expert", "dp", None, None),
            P("expert", "dp", None, None),
        ),
        out_specs=(
            P(("dp", "expert"), None),
            P("expert", "dp", None, None),
            P("expert", "dp", None, None),
        ),
        check_vma=False,
    )
```

time: 224 us -> 214 us (0.955)
  matrix products: 9.94 us -> 0 us
  starting transfers between devices: 9.48 us -> 0 us
  Pallas kernels: 192 us -> 197 us
  other arithmetic: 3.3 us -> 8 us
    dot_general x6 -> x0, matrix products: 9.94 us -> none  [the longest x1 2.75 us: per_device(): lax.dot_general(rows_x, gate_up, contract_last, preferred_element_type=jn...]
    ppermute x2 -> x0, starting transfers between devices: 9.48 us -> none  [half_swap(): return lax.ppermute(block, 'expert', route)]
    pallas_call x3 -> x1, Pallas kernels: 192 us -> 197 us  [whole_step(): pl.pallas_call(functools.partial(step_kernel, n_cols), out_shape=(jax.Sha...]
    reshape x5 -> x0, local copies, waits for them, and re-layouts: 4.48 us -> none  [the longest x3 2.78 us: per_device(): back.reshape(slots, n_cols, CAP, width).transpose(1, 0, 2, 3)]
    reshape x0 -> x2, other arithmetic: none -> 4.1 us  [the longest x1 2.1 us: per_device(): jnp.where(came, far[:gate_up_rows], near[:gate_up_rows])]
    unnamed x19 -> x8, local copies, waits for them, and re-layouts: 0.31 us -> 2.9 us
  transfers between devices with their start and end apart: 2 -> 0, of which waited for: 0 -> 0; matrix products, arithmetic and copies ran while one was open for 4% -> 0% of each run, Pallas kernels for 86% -> 0%
where the time goes in v4:
time: 214 us
  Pallas kernels  197 us (92%)
  other arithmetic  8 us (4%)
  local copies, waits for them, and re-layouts  6.76 us (3%)
    pallas_call x1, Pallas kernels, whole_step(): pl.pallas_call(functools.partial(step_kernel, n_cols), out_shape=(jax.Sha...  197 us

profile of v4, /device:TPU:1, one launch (start us, length us, event | category | flops | bytes accessed | tf_op | source)
XLA Modules:
  0.0 213.7 jit_solution(5311910805578644704)
XLA Ops:
  0.7 0.8 select_reduce_fusion.2
  1.5 0.6 fusion.17
  3.4 0.1 select_reduce_fusion.1
  3.5 0.7 convert_element_type.35
  4.2 0.1 copy.40
  4.3 0.6 broadcast_in_dim.75.flag_ref
  4.9 0.6 broadcast_in_dim.73.lane_ref
  5.5 0.7 reduce_precision.6
  6.2 0.1 copy.37
  6.2 0.8 copy.41
  7.0 0.1 eq.98
  7.1 0.8 copy.38
  7.9 0.8 copy.46
  8.6 0.1 broadcast_in_dim.76
  8.7 0.2 select_reduce_fusion
  8.9 0.1 mul.54
  9.0 0.1 reduce_sum.64
  9.1 0.1 fusion.14
  9.1 0.7 fusion.1.picks_ref
  9.9 0.7 broadcast_in_dim.74.row_ref
  10.6 1.5 concatenate.3.own_ref
  12.1 196.9 %whole_step.1 = (bf16[16,1024]{1,0:T(8,128)(2,1)}, bf16[576,1024]{1,0:T(8,128)(2,1)}, bf16[576,1024]{1,0:T(8,128)(2,1)}) custom-call(bf16[16,2176]{1,0:T(8,128)(2,1)} %concatenate.3.own_ref, f32[8,128]{1,0:T(8,128)} %broadcast_in_dim.73.lane_ref, f32[64,128]{1,0:T(8,128)} %broadcast_in_dim.74.row_ref, f32[8,128]{1,0:T(8,128)} %broadcast_in_dim.75.flag_ref, ...), custom_call_target="tpu_custom_call" | custom-call | tf_op jit(solution)/shard_map/whole_step/pallas_call | solution.py:447
  208.9 0.0 copy-start
  209.0 2.0 select_bitcast_fusion.1
  211.0 0.0 copy-done
  211.0 0.0 copy-start.1
  211.0 2.1 select_bitcast_fusion
  213.1 0.0 copy-done.1
  213.1 0.6 copy.48
  (7 shorter events, 0.0 us)
Async XLA Ops:
  208.9 2.0 copy-start
  211.0 2.1 copy-start.1

commit v5 on v4

--- a/solution.py
+++ b/solution.py
@@ -19,27 +19,6 @@
 def silu_parts(values_in):
     sigmoid_of = jax.nn.sigmoid(values_in)
     return (values_in * sigmoid_of, sigmoid_of * (1.0 + values_in * (1.0 - sigmoid_of)))
-
-
-def half_swap(block, count, parity):
-    half = count // 2
-    route = [(c, (c + half) % count) for c in range(count) if c % 2 == parity]
-    return lax.ppermute(block, "expert", route)
-
-
-def three_parts(gates):
-    first = lax.reduce_precision(gates, 8, 7)
-    rest = gates - first
-    second = lax.reduce_precision(rest, 8, 7)
-    third = rest - second
-    return [part.astype(jnp.bfloat16) for part in (first, second, third)]
-
-
-def meet(peers):
-    barrier = pltpu.get_barrier_semaphore()
-    for peer in peers:
-        pl.semaphore_signal(barrier, inc=1, device_id=peer, device_id_type=MESH)
-    pl.semaphore_wait(barrier, len(peers))
 
 
 def remote(src, dst, send_sem, recv_sem, peer):
@@ -97,15 +76,15 @@
 
 
 def moves_weights(e):
-    return lax.rem(e, 2) == 0
+    return (lax.rem(e, 2) == 0) & (lax.rem(e // 2, 4) < 3)
 
 
 def step_kernel(
-    n_cols, own_ref, lane_ref, row_ref, flag_ref, picks_ref, gate_up_ref, down_ref,
-    tokens_ref, grads_ref, far_grads,
-    held, sent, rows_in, weights, far_weights, da_all, db_all, hidden_all,
+    n_cols, own_tokens, own_upstream, ids_ref, gates_ref, moves_ref, gate_up_ref, down_ref,
+    tokens_ref, grad_gate_up_ref, grad_down_ref,
+    own_ref, far_grads, held, sent, rows_in, weights, far_weights, da_all, db_all, hidden_all,
     part_ref, relay, summed, got, total, back, places, home,
-    keep_sem, send_p, recv_p, send_m, recv_m, send_s, recv_s,
+    keep_sem, send_p2, recv_p2, send_p1, recv_p1, send_m2, recv_m2, send_m1, recv_m1, send_s, recv_s,
     keep_x, send_x, recv_x, send_y, recv_y, send_f, recv_f,
     load_w, send_w, recv_w, send_g, recv_g,
     send_r, recv_r, send_d, recv_d, send_t, recv_t, send_b, recv_b, keep_b,
@@ -117,8 +96,9 @@
     chip, core = e // 2, lax.rem(e, 2)
     my_x, my_y, at = xy_peers()
     north, south = at(0, 1), at(0, 3)
-    ahead = {"expert": lax.rem(e + 2, n_cols)}
-    behind = {"expert": lax.rem(e + n_cols - 2, n_cols)}
+    ahead, behind = [
+        [{"expert": lax.rem(e + sign * 2 * hops + n_cols, n_cols)} for hops in (1, 2)] for sign in (1, -1)
+    ]
     twin = {"expert": e + 1 - 2 * core}
     across = {"expert": lax.rem(e + chips, n_cols)}
     tok_dev, full = own_ref.shape
@@ -128,12 +108,9 @@
     block_rows = SLICES * slots * seats
     per_group = seats // CAP
     f_slice = down_ref.shape[0]
-    quarter = width // 2
-    cuts = [
-        pl.ds(0, quarter), pl.ds(quarter, quarter), pl.ds(2 * quarter, quarter), pl.ds(3 * quarter, quarter + 128)
-    ]
+    cuts = [pl.ds(0, width), pl.ds(width, width + 128)]
     n_cut = len(cuts)
-    up_steps, down_steps = chips // 2, chips // 2 - 1
+    relays = chips // 4
     early = moves_weights(e)
 
     def peer(place):
@@ -144,7 +121,70 @@
         shift = -order[place // 2]
         return order.index(shift if shift < chips // 2 else -shift) * 2 + place % 2
 
-    meet([peer(place) for place in range(1, n_cols)] + [at(1, 0), at(2, 0), at(3, 0), north, south])
+    peers = [peer(place) for place in range(1, n_cols)] + [at(1, 0), at(2, 0), at(3, 0), north, south]
+    barrier = pltpu.get_barrier_semaphore()
+    for other in peers:
+        pl.semaphore_signal(barrier, inc=1, device_id=other, device_id_type=MESH)
+
+    def iota(shape, axis):
+        return lax.broadcasted_iota(jnp.int32, shape, axis)
+
+    def as_f32(mask):
+        return jnp.where(mask, 1.0, 0.0)
+
+    def expert_of(column, slot, relocated, moves):
+        column = column + chips * relocated * moves
+        return (column - n_cols * as_f32(column >= n_cols)) * slots + slot
+
+    top = ids_ref.shape[0]
+    own_ref[:, 0:width] = own_tokens[...]
+    own_ref[:, width : 2 * width] = own_upstream[...]
+    gates = gates_ref[...]
+    first = gates.astype(jnp.bfloat16).astype(jnp.float32)
+    second = (gates - first).astype(jnp.bfloat16).astype(jnp.float32)
+    third = gates - first - second
+    columns = jnp.concatenate([ids_ref[...].astype(jnp.float32), first, second, third], axis=0)
+    spread_out = as_f32(iota((4 * top, 128), 0) == iota((4 * top, 128), 1))
+    meta = lax.dot_general(columns, spread_out, contract_first, preferred_element_type=jnp.float32)
+    own_ref[:, 2 * width :] = meta.astype(jnp.bfloat16)
+    moves = moves_ref[...].astype(jnp.float32)
+    here = iota((slots, n_cols), 1) == e
+    relocated_here = jnp.sum(jnp.where(here, moves, 0.0), axis=1, keepdims=True)
+    flag = jnp.sum(
+        jnp.where(iota((slots, 1), 0) == my_x, relocated_here, 0.0), axis=0, keepdims=True
+    )
+    served = expert_of(
+        jnp.full((slots, 1), e, jnp.int32).astype(jnp.float32), iota((slots, 1), 0).astype(jnp.float32),
+        relocated_here, jnp.where(early, 1.0, 0.0),
+    )
+    lane_ids = jnp.sum(
+        jnp.where(iota((slots, 128), 1) // seats == iota((slots, 128), 0), served, 0.0), axis=0, keepdims=True
+    ) - as_f32(iota((1, 128), 1) >= slots * seats)
+    row_of = iota((slots * seats, 128), 0) // seats
+    row_ids = sum(jnp.where(row_of == q, served[q : q + 1], 0.0) for q in range(slots))
+    per_place = slots * CAP
+    n_home = n_cols * per_place
+    lane = iota((1, n_home), 1)
+    index, rest = lane // (2 * per_place), lane // per_place % 2
+    shift = jnp.where(index % 2 == 1, (index + 1) // 2, -(index // 2))
+    column = 2 * lax.rem(chip + shift + chips, chips) + jnp.where(rest == 0, core, 1 - core)
+    slot = lane // CAP % slots
+    moved_there = jnp.dot(
+        moves, as_f32(iota((n_cols, n_home), 0) == column), preferred_element_type=jnp.float32
+    )
+    moved_there = jnp.sum(
+        jnp.where(iota((slots, n_home), 0) == slot, moved_there, 0.0), axis=0, keepdims=True
+    )
+    from_expert = expert_of(
+        column.astype(jnp.float32), slot.astype(jnp.float32), moved_there, as_f32(moves_weights(column))
+    )
+    named = meta[:, 0:1] == from_expert
+    for k in range(1, top):
+        named = named | (meta[:, k : k + 1] == from_expert)
+    before = as_f32(iota((tok_dev, tok_dev), 1) < iota((tok_dev, tok_dev), 0))
+    ranks = jnp.dot(before, as_f32(named), preferred_element_type=jnp.float32)
+    picks = as_f32(named & (ranks == (lane % CAP).astype(jnp.float32))).astype(jnp.bfloat16)
+    pl.semaphore_wait(barrier, len(peers))
     started = []
 
     def go(copy):
@@ -161,11 +201,13 @@
     def source(shift, h):
         return own_ref.at[:, cuts[h]] if shift == 0 else spot(shift, 0, h)
 
-    def up(s, h):
-        return remote(source(-s, h), spot(-(s + 1), 0, h), send_p.at[s, h], recv_p.at[s, h], ahead)
-
-    def down(s, h):
-        return remote(source(s, h), spot(s + 1, 0, h), send_m.at[s, h], recv_m.at[s, h], behind)
+    def up(hops, r, h):
+        send, recv = ((send_p1, recv_p1), (send_p2, recv_p2))[hops - 1]
+        return remote(source(-2 * r, h), spot(-2 * r - hops, 0, h), send.at[r, h], recv.at[r, h], ahead[hops - 1])
+
+    def down(hops, r, h):
+        send, recv = ((send_m1, recv_m1), (send_m2, recv_m2))[hops - 1]
+        return remote(source(2 * r, h), spot(2 * r + hops, 0, h), send.at[r, h], recv.at[r, h], behind[hops - 1])
 
     def side(shift, h):
         index = order.index(shift)
@@ -213,7 +255,7 @@
             if index % 2 == 1:
                 for h in range(n_cut):
                     side(order[index // 2], h).wait_recv()
-        x_rows, d_rows = pick_rows(held[g], lane_ref[0:1, :], row_ref[...], tok_dev, seats)
+        x_rows, d_rows = pick_rows(held[g], lane_ids, row_ids, tok_dev, seats)
         for q in range(slots):
             sent[g, q, :, 0:width] = x_rows[q * seats : (q + 1) * seats]
             sent[g, q, :, width : 2 * width] = d_rows[q * seats : (q + 1) * seats]
@@ -224,9 +266,11 @@
         keep.start()
         keeps.append(keep)
 
+    for hops in (2, 1):
+        for h in range(n_cut):
+            go(up(hops, 0, h))
+            go(down(hops, 0, h))
     for h in range(n_cut):
-        go(up(0, h))
-        go(down(0, h))
         go(side(0, h))
     own = pltpu.make_async_copy(own_ref, held.at[0, pl.ds(0, tok_dev)], keep_sem)
     own.start()
@@ -238,20 +282,29 @@
     for load in loads:
         load.start()
     own.wait()
-    for s in range(1, up_steps + 1):
+    for r in range(1, relays + 1):
+        more = r < relays
         for h in range(n_cut):
-            up(s - 1, h).wait_recv()
-            if s < up_steps:
-                go(up(s, h))
-            if s <= down_steps:
-                down(s - 1, h).wait_recv()
-                if s < down_steps:
-                    go(down(s, h))
+            up(2, r - 1, h).wait_recv()
+            if more:
+                go(up(2, r, h))
+                down(2, r - 1, h).wait_recv()
+                if r < relays - 1:
+                    go(down(2, r, h))
+        if more:
+            for h in range(n_cut):
+                go(up(1, r, h))
+                go(down(1, r, h))
         for h in range(n_cut):
-            go(side(-s, h))
-            if s <= down_steps:
-                go(side(s, h))
-        if s == up_steps:
+            go(side(-2 * r, h))
+            if more:
+                go(side(2 * r, h))
+        for h in range(n_cut):
+            up(1, r - 1, h).wait_recv()
+            go(side(1 - 2 * r, h))
+            down(1, r - 1, h).wait_recv()
+            go(side(2 * r - 1, h))
+        if r == relays:
             w_copies = [
                 remote(gate_up_ref, far_weights.at[gate_up_at], send_w.at[0], recv_w.at[0], across),
                 remote(down_ref, far_weights.at[down_at], send_w.at[1], recv_w.at[1], across),
@@ -262,13 +315,11 @@
                 for copy in w_copies:
                     copy.start()
 
-        if s % 2 == 0:
-            choose(s // 2 - 1)
-        elif s > 1:
-            g = (s - 3) // 2
-            x_then_y(g)
-            if g > 0:
-                pass_on(g - 1)
+        choose(r - 1)
+        if r >= 2:
+            x_then_y(r - 2)
+        if r >= 3:
+            pass_on(r - 3)
     last = groups - 1
     pass_on(last - 1)
     x_then_y(last)
@@ -284,7 +335,7 @@
     def _():
         for copy in w_copies:
             copy.wait()
-        moved = jnp.broadcast_to(flag_ref[0:1, 0:1], (f_slice, width)) > 0.5
+        moved = jnp.broadcast_to(flag, (f_slice, width)) > 0.5
         for i in range(3):
             at_rows = pl.ds(i * f_slice, f_slice)
             weights[at_rows] = jnp.where(
@@ -310,15 +361,17 @@
 
     lax.fori_loop(0, groups, forward, 0)
     every_row = rows_in[...].reshape(groups * block_rows, 2 * width)
-    g_copies = []
+    g_copies, g_places = [], []
     for i, (left, lo) in enumerate(((da_all, 0), (db_all, 0), (hidden_all, width))):
         at_rows = pl.ds(i * f_slice, f_slice)
-        grads_ref[at_rows] = lax.dot_general(
+        out_ref, out_rows = ((grad_gate_up_ref, at_rows), (grad_down_ref, pl.ds(0, f_slice)))[i // 2]
+        out_ref[out_rows] = lax.dot_general(
             left[...].reshape(groups * block_rows, f_slice), every_row[:, lo : lo + width], contract_first,
             preferred_element_type=jnp.float32,
         ).astype(jnp.bfloat16)
+        g_places.append((out_ref, out_rows, at_rows))
         g_copies.append(
-            remote(grads_ref.at[at_rows], far_grads.at[at_rows], send_g.at[i], recv_g.at[i], across)
+            remote(out_ref.at[out_rows], far_grads.at[at_rows], send_g.at[i], recv_g.at[i], across)
         )
 
     @pl.when(jnp.logical_not(early))
@@ -367,7 +420,6 @@
             go(total_copy(g, way, i))
     back_keeps = []
 
-    per_place = slots * CAP
     n_rows = slots * seats
     to_row = lax.broadcasted_iota(jnp.int32, (n_rows, n_rows), 0)
     from_row = lax.broadcasted_iota(jnp.int32, (n_rows, n_rows), 1)
@@ -417,39 +469,48 @@
     for place in range(1, n_cols):
         landed(home.at[place], send_h.at[place], recv_h.at[place], peer(place))
     tokens_ref[...] = jnp.dot(
-        picks_ref[...], home[...].reshape(n_cols * per_place, width), preferred_element_type=jnp.float32
+        picks, home[...].reshape(n_cols * per_place, width), preferred_element_type=jnp.float32
     ).astype(tokens_ref.dtype)
 
     @pl.when(jnp.logical_not(early))
     def _():
         for copy in g_copies:
             copy.wait()
+        came = jnp.broadcast_to(flag, (f_slice, width)) > 0.5
+        for out_ref, out_rows, at_rows in g_places:
+            out_ref[out_rows] = jnp.where(
+                came, far_grads[at_rows].astype(jnp.float32), out_ref[out_rows].astype(jnp.float32)
+            ).astype(jnp.bfloat16)
 
     for copy in started:
         copy.wait_send()
 
 
-def whole_step(packed, lane_ids, row_ids, flag, picks, gate_up, down, n_cols, slots):
-    tok_dev, full = packed.shape
+def whole_step(tokens, upstream, ids, gates, moves, gate_up, down):
+    tok_dev, width = tokens.shape
+    slots, n_cols = moves.shape
+    full = 2 * width + 128
     chips = n_cols // 2
     groups = 4
     seats = n_cols * CAP // groups
-    width = (full - 128) // 2
     f_slice = down.shape[0]
     block_rows = SLICES * slots * seats
     pair = SLICES // 2
-    up, down_steps = chips // 2, chips // 2 - 1
-    cut = 4
+    relays = chips // 4
+    cut = 2
     bf16 = jnp.bfloat16
     dma = pltpu.SemaphoreType.DMA
     any_spec = pl.BlockSpec(memory_space=pl.ANY)
-    grads = jax.ShapeDtypeStruct((3 * f_slice, width), bf16)
     return pl.pallas_call(
         functools.partial(step_kernel, n_cols),
-        out_shape=(jax.ShapeDtypeStruct((tok_dev, width), bf16), grads, grads),
+        out_shape=tuple(
+            jax.ShapeDtypeStruct((rows, width), bf16) for rows in (tok_dev, 2 * f_slice, f_slice)
+        ),
         in_specs=[VMEM_SPEC] * 5 + [any_spec] * 2,
         out_specs=(VMEM_SPEC,) * 3,
         scratch_shapes=[
+            pltpu.VMEM((tok_dev, full), bf16),
+            pltpu.VMEM((3 * f_slice, width), bf16),
             pltpu.VMEM((groups, n_cols // groups * tok_dev, full), bf16),
             pltpu.VMEM((groups, slots, seats, 2 * width), bf16),
             pltpu.VMEM((groups, SLICES, slots, seats, 2 * width), bf16),
@@ -466,7 +527,8 @@
             pltpu.VMEM((groups, slots, seats, width), bf16),
             pltpu.VMEM((n_cols, slots * CAP, width), bf16),
             pltpu.VMEM((n_cols, slots * CAP, width), bf16),
-            dma, dma((up, cut)), dma((up, cut)), dma((down_steps, cut)), dma((down_steps, cut)),
+            dma,
+        ] + [dma((relays, cut))] * 8 + [
             dma((chips, cut)), dma((chips, cut)),
             dma((groups,)), dma((groups, SLICES)), dma((groups, SLICES)),
             dma((groups, 2, SLICES)), dma((groups, 2, SLICES)),
@@ -480,73 +542,14 @@
             collective_id=0, has_side_effects=True, vmem_limit_bytes=56 * 1024 * 1024
         ),
         name="whole_step",
-    )(packed, lane_ids, row_ids, flag, picks, gate_up, down)
+    )(tokens, upstream, ids, gates, moves, gate_up, down)
 
 
 def per_device(tokens, upstream, expert_ids, gates, relocate, w_gate_up, w_down):
-    n_rows = lax.axis_size("dp")
-    n_cols = lax.axis_size("expert")
-    slots = n_rows // SLICES
-    tok_dev, width = tokens.shape
-    top = expert_ids.shape[1]
-    slice_width = w_down.shape[2]
-    half = n_cols // 2
-    seats = n_cols * CAP
-    col = lax.axis_index("expert")
-    slot_here = lax.axis_index("dp") // SLICES
-
-    meta = jnp.concatenate(
-        [expert_ids.astype(jnp.bfloat16)] + three_parts(gates)
-        + [jnp.zeros((tok_dev, 128 - 4 * top), jnp.bfloat16)],
-        axis=1,
-    )
-    packed = jnp.concatenate([tokens, upstream, meta], axis=1)
-    early = moves_weights(col)
-    rel_row = jnp.sum(
-        jnp.where(jnp.arange(n_cols)[:, None] == col, relocate, 0), axis=0
-    )
-    served = jnp.where(early, (col + half * rel_row) % n_cols, col) * slots + jnp.arange(slots)
-    group_seats = seats // 4
-    lanes = jnp.arange(128, dtype=jnp.int32) // group_seats
-    lane_ids = jnp.sum(
-        jnp.where(lanes[None, :] == jnp.arange(slots)[:, None], served[:, None] + 1, 0), axis=0
-    ) - 1
-    lane_ids = lane_ids.astype(jnp.float32)
-    row_ids = jnp.broadcast_to(lane_ids[: slots * group_seats, None], (slots * group_seats, 128))
-    lane_ids = jnp.broadcast_to(lane_ids[None, :], (8, 128))
-    rel_here = jnp.sum(jnp.where(jnp.arange(slots) == slot_here, rel_row, 0))
-
-    flat_ids = expert_ids.reshape(-1)
-    experts = slots * n_cols
-    relocated = jnp.sum(
-        jnp.where(flat_ids[:, None] == jnp.arange(experts)[None, :], relocate.reshape(1, experts), 0), axis=1
-    )
-    home_col = flat_ids // slots
-    served_col = jnp.where(moves_weights(home_col), (home_col + half * relocated) % n_cols, home_col)
-    token_of = jnp.arange(flat_ids.shape[0], dtype=jnp.int32) // top
-    earlier = (flat_ids[:, None] == flat_ids[None, :]) & (token_of[None, :] < token_of[:, None])
-    rank = jnp.sum(earlier.astype(jnp.int32), axis=1)
-    chips = n_cols // 2
-    shift = (served_col // 2 - col // 2 + chips // 2 + chips) % chips - chips // 2
-    place = jnp.minimum(jnp.where(shift > 0, 2 * shift - 1, -2 * shift), chips - 1) * 2
-    place = place + (served_col % 2 != col % 2).astype(jnp.int32)
-    target = ((place * slots + flat_ids % slots) * CAP + rank).reshape(tok_dev, top)
-    n_home = n_cols * slots * CAP
-    picks = jnp.sum(
-        (target[:, :, None] == jnp.arange(n_home, dtype=jnp.int32)[None, None, :]).astype(jnp.bfloat16),
-        axis=1,
-    )
-    flag = jnp.broadcast_to(rel_here.astype(jnp.float32), (8, 128))
-    grad_tokens, near, far = whole_step(
-        packed, lane_ids, row_ids, flag, picks, w_gate_up[0, 0], w_down[0, 0], n_cols, slots
-    )
-    came = ~early & (rel_here == 1)
-    gate_up_rows = 2 * slice_width
-    return (
-        grad_tokens,
-        jnp.where(came, far[:gate_up_rows], near[:gate_up_rows]).reshape(w_gate_up.shape),
-        jnp.where(came, far[gate_up_rows:], near[gate_up_rows:]).reshape(w_down.shape),
-    )
+    grad_tokens, grad_gate_up, grad_down = whole_step(
+        tokens, upstream, expert_ids.T, gates.T, relocate.T, w_gate_up[0, 0], w_down[0, 0]
+    )
+    return (grad_tokens, grad_gate_up.reshape(w_gate_up.shape), grad_down.reshape(w_down.shape))
 
 
 def solution(mesh):

time: 214 us -> 192 us (0.90)
  Pallas kernels: 197 us -> 186 us
  other arithmetic: 8 us -> 0 us
  local copies, waits for them, and re-layouts: 6.76 us -> 4.24 us
    pallas_call x1, Pallas kernels: 197 us -> 186 us  [whole_step(): pl.pallas_call(functools.partial(step_kernel, n_cols), out_shape=tuple((j...]
    reshape x2 -> x0, other arithmetic: 4.1 us -> none  [the longest x1 2.1 us: per_device(): jnp.where(came, far[:gate_up_rows], near[:gate_up_rows])]
    reduce_sum x5 -> x0, other arithmetic: 2.42 us -> none  [the longest x1 0.8 us: per_device(): jnp.sum(jnp.where(jnp.arange(n_cols)[:, None] == col, relocate, 0), axis=0)]
where the time goes in v5:
time: 192 us; the launch traced here: 191 us
  Pallas kernels  186 us (97%)
  local copies, waits for them, and re-layouts  4.24 us (2%)
    pallas_call x1, Pallas kernels, whole_step(): pl.pallas_call(functools.partial(step_kernel, n_cols), out_shape=tuple((j...  186 us
    unnamed x5, local copies, waits for them, and re-layouts  4.24 us

profile of v5, /device:TPU:1, one launch (start us, length us, event | category | flops | bytes accessed | tf_op | source)
XLA Modules:
  0.0 191.2 jit_solution(13380425550319147361)
XLA Ops:
  0.6 186.4 %whole_step.1 = (bf16[16,1024]{1,0:T(8,128)(2,1)}, bf16[384,1024]{1,0:T(8,128)(2,1)}, bf16[192,1024]{1,0:T(8,128)(2,1)}) custom-call(bf16[16,1024]{1,0:T(8,128)(2,1)} %own_tokens.1, bf16[16,1024]{1,0:T(8,128)(2,1)} %own_upstream.1, s32[8,16]{1,0:T(8,128)} %bitcast.11, f32[8,16]{1,0:T(8,128)} %bitcast.12, s32[4,32]{1,0:T(4,128)} %bitcast.13, ...), custom_call_target="tpu_custom_call" | custom-call | tf_op jit(solution)/shard_map/whole_step/pallas_call | solution.py:504
  187.0 1.4 copy.13
  188.4 0.0 copy-start
  188.4 2.1 %copy.14 = bf16[1,1,384,1024]{3,2,1,0:T(8,128)(2,1)} copy(bf16[1,1,384,1024]{3,2,1,0:T(8,128)(2,1)} %bitcast.8) | data formatting | bytes 1572864
  190.5 0.0 copy-done
  190.5 0.7 copy.15
Async XLA Ops:
  188.4 2.1 %copy-start = (bf16[192,1024]{1,0:T(8,128)(2,1)S(1)}, bf16[192,1024]{1,0:T(8,128)(2,1)}, u32[]{:S(2)}) copy-start(bf16[192,1024]{1,0:T(8,128)(2,1)} %get-tuple-element.8) | copy-start | bytes 1179652

commit v6 on v5

--- a/solution.py
+++ b/solution.py
@@ -76,7 +76,7 @@
 
 
 def moves_weights(e):
-    return (lax.rem(e, 2) == 0) & (lax.rem(e // 2, 4) < 3)
+    return (lax.rem(e, 2) == 0) & (lax.rem(e // 2, 8) < 6)
 
 
 def step_kernel(
@@ -374,9 +374,8 @@
             remote(out_ref.at[out_rows], far_grads.at[at_rows], send_g.at[i], recv_g.at[i], across)
         )
 
-    @pl.when(jnp.logical_not(early))
-    def _():
-        for copy in g_copies:
+        @pl.when(jnp.logical_not(early))
+        def _(copy=g_copies[-1]):
             copy.start()
 
     pair = SLICES // 2

time: 192 us -> 179 us (0.932)
  Pallas kernels: 186 us -> 174 us
    pallas_call x1, Pallas kernels: 186 us -> 174 us  [whole_step(): pl.pallas_call(functools.partial(step_kernel, n_cols), out_shape=tuple((j...]
where the time goes in v6:
time: 179 us
  Pallas kernels  174 us (97%)
  local copies, waits for them, and re-layouts  4.24 us (2%)
    pallas_call x1, Pallas kernels, whole_step(): pl.pallas_call(functools.partial(step_kernel, n_cols), out_shape=tuple((j...  174 us
    unnamed x5, local copies, waits for them, and re-layouts  4.24 us

profile of v6, /device:TPU:1, one launch (start us, length us, event | category | flops | bytes accessed | tf_op | source)
XLA Modules:
  0.0 179.2 jit_solution(4992290776366813540)
XLA Ops:
  0.6 174.3 %whole_step.1 = (bf16[16,1024]{1,0:T(8,128)(2,1)}, bf16[384,1024]{1,0:T(8,128)(2,1)}, bf16[192,1024]{1,0:T(8,128)(2,1)}) custom-call(bf16[16,1024]{1,0:T(8,128)(2,1)} %own_tokens.1, bf16[16,1024]{1,0:T(8,128)(2,1)} %own_upstream.1, s32[8,16]{1,0:T(8,128)} %bitcast.11, f32[8,16]{1,0:T(8,128)} %bitcast.12, s32[4,32]{1,0:T(4,128)} %bitcast.13, ...), custom_call_target="tpu_custom_call" | custom-call | tf_op jit(solution)/shard_map/whole_step/pallas_call | solution.py:503
  174.9 1.4 copy.13
  176.3 0.0 copy-start
  176.3 2.1 %copy.14 = bf16[1,1,384,1024]{3,2,1,0:T(8,128)(2,1)} copy(bf16[1,1,384,1024]{3,2,1,0:T(8,128)(2,1)} %bitcast.8) | data formatting | bytes 1572864
  178.4 0.0 copy-done
  178.4 0.7 copy.15
Async XLA Ops:
  176.3 2.1 %copy-start = (bf16[192,1024]{1,0:T(8,128)(2,1)S(1)}, bf16[192,1024]{1,0:T(8,128)(2,1)}, u32[]{:S(2)}) copy-start(bf16[192,1024]{1,0:T(8,128)(2,1)} %get-tuple-element.8) | copy-start | bytes 1179652

commit v7 on v6

--- a/solution.py
+++ b/solution.py
@@ -374,7 +374,7 @@
             remote(out_ref.at[out_rows], far_grads.at[at_rows], send_g.at[i], recv_g.at[i], across)
         )
 
-        @pl.when(jnp.logical_not(early))
+        @pl.when(jnp.logical_not(early) & (i < 2))
         def _(copy=g_copies[-1]):
             copy.start()
 
@@ -462,6 +462,11 @@
         if g > 0:
             send_home(g - 1)
     send_home(groups - 1)
+
+    @pl.when(jnp.logical_not(early))
+    def _():
+        g_copies[2].start()
+
     keep = pltpu.make_async_copy(places.at[0], home.at[0], keep_h)
     keep.start()
     keep.wait()

time: 179 us -> 177 us (0.989)
  the two profiles are of different devices: /device:TPU:1 before, /device:TPU:167 now
where the time goes in v7:
time: 177 us
  Pallas kernels  172 us (97%)
  local copies, waits for them, and re-layouts  4.24 us (2%)
    pallas_call x1, Pallas kernels, whole_step(): pl.pallas_call(functools.partial(step_kernel, n_cols), out_shape=tuple((j...  172 us
    unnamed x5, local copies, waits for them, and re-layouts  4.24 us

profile of v7, /device:TPU:167, one launch (start us, length us, event | category | flops | bytes accessed | tf_op | source)
XLA Modules:
  0.0 176.8 jit_solution(17690544853179171000)
XLA Ops:
  0.6 172.0 %whole_step.1 = (bf16[16,1024]{1,0:T(8,128)(2,1)}, bf16[384,1024]{1,0:T(8,128)(2,1)}, bf16[192,1024]{1,0:T(8,128)(2,1)}) custom-call(bf16[16,1024]{1,0:T(8,128)(2,1)} %own_tokens.1, bf16[16,1024]{1,0:T(8,128)(2,1)} %own_upstream.1, s32[8,16]{1,0:T(8,128)} %bitcast.11, f32[8,16]{1,0:T(8,128)} %bitcast.12, s32[4,32]{1,0:T(4,128)} %bitcast.13, ...), custom_call_target="tpu_custom_call" | custom-call | tf_op jit(solution)/shard_map/whole_step/pallas_call | solution.py:508
  172.6 1.4 copy.13
  174.0 0.0 copy-start
  174.0 2.1 %copy.14 = bf16[1,1,384,1024]{3,2,1,0:T(8,128)(2,1)} copy(bf16[1,1,384,1024]{3,2,1,0:T(8,128)(2,1)} %bitcast.8) | data formatting | bytes 1572864
  176.1 0.0 copy-done
  176.1 0.7 copy.15
Async XLA Ops:
  174.0 2.1 %copy-start = (bf16[192,1024]{1,0:T(8,128)(2,1)S(1)}, bf16[192,1024]{1,0:T(8,128)(2,1)}, u32[]{:S(2)}) copy-start(bf16[192,1024]{1,0:T(8,128)(2,1)} %get-tuple-element.8) | copy-start | bytes 1179652
